TPU v7x, 512 devices: a whole 4x4x16 slice. The times are simulated.
512 devices in a mesh: space: 32 (over z_hi, x, y), tm: 16 (over z_lo, core).
Axes of the slice: x: 4, y: 4, z: 16 (z_hi: 2, z_lo: 8; z = z_hi * 8 + z_lo), core: 2. Of those that a mesh axis runs over, the one named last changes fastest.
Arguments:
- concentration: float32 [64, 128, 128], P('space'), may hold values from 0 to 2
- velocity: bfloat16 [3, 64, 128, 128], P(None, 'space'), may hold values from -0.29882812 to 0.29882812
- porosity: float32 [64, 128, 128], P('space'), may hold values from 0.15 to 0.4
- contacts: int32 [512, 4], P('space'), may hold values from 0 to 32767
- sources: int32 [32, 2], P('tm'), may hold values from 0 to 511
- receivers: int32 [32, 64, 2], P('tm'), may hold values from 0 to 511, all different within a row
- observed: float32 [32, 64], P('tm'), may hold values from -6 to 6
- potential_init: float32 [32, 64, 128, 128], P('tm', 'space'), may hold values from -12 to 12
- adjoint_init: float32 [32, 64, 128, 128], P('tm', 'space'), may hold values from -12 to 12
Outputs:
- gradient: float32 [64, 128, 128], P('space')
- readings: float32 [32, 64], P('tm')
Inputs may be any that keep to these rules, and one draw needn't show every extreme that they name: contacts[e, c] indexes the flattened cells of tile e // 16, which holds electrode e. `sources`: electrode ids. `receivers`: the two electrodes of a receiver pair differ.
All inputs are finite; a program needn't handle non-finite values.
Results may differ from a plain program's by a relative error of at most 0.0003.
Values sent between devices are 32-bit elements; how exact they have to be, the bound alone decides.
A program may use at most 64 MiB of HBM per device.

v0:
```python
import jax
import jax.numpy as jnp
from jax import lax
from jax.sharding import PartitionSpec as P

CONTACTS = 4
STEPS = 8
RELAX_SWEEPS = 6


archie_exponent = 1.8
water_conductivity = 0.5
relaxation = 0.8
injected_current = 4.0


def extended(block, sides, width):
    for axis, dim in sides:
        count = lax.axis_size(axis)
        forward = [(i, i + 1) for i in range(count - 1)]
        backward = [(target, source) for source, target in forward]
        low = lax.ppermute(
            lax.slice_in_dim(block, block.shape[dim] - width, None, axis=dim), axis, forward
        )
        high = lax.ppermute(lax.slice_in_dim(block, 0, width, axis=dim), axis, backward)
        block = jnp.concatenate([low, block, high], axis=dim)
    return block


def passed_along(block, axis, distance):
    devices = range(lax.axis_size(axis))
    route = [(i - distance, i) for i in devices if i - distance in devices]
    return lax.ppermute(block, axis, route)


def behind(values, along):
    widths = [(0, 0)] * values.ndim
    widths[along] = (1, 0)
    return lax.slice_in_dim(jnp.pad(values, widths), 0, values.shape[along], axis=along)


def beyond(values, along):
    widths = [(0, 0)] * values.ndim
    widths[along] = (0, 1)
    return lax.slice_in_dim(jnp.pad(values, widths), 1, values.shape[along] + 1, axis=along)


def harmonic(first, second):
    return 2.0 * (first * second) / (first + second)


def advect(tracer, speeds, neighbours):
    change = jnp.zeros_like(tracer)
    for dim_index in range(3):
        speed = speeds[dim_index]
        lowside, highside = neighbours[dim_index]
        change = (
            change
            + jnp.maximum(speed, 0.0) * (tracer - lowside)
            + jnp.minimum(speed, 0.0) * (highside - tracer)
        )
    return tracer - change


def archie(porosity, tracer):
    return jnp.exp(archie_exponent * jnp.log(porosity)) * (water_conductivity + tracer)


def on_device(
    concentration,
    velocity,
    porosity,
    contacts,
    sources,
    receivers,
    observed,
    potential_init,
    adjoint_init,
):
    speeds = velocity.astype(jnp.float32)
    tracer = concentration
    for _ in range(STEPS):
        padded = extended(tracer, (("space", 0),), 1)
        neighbours = [
            (padded[:-2], padded[2:]),
            (behind(tracer, 1), beyond(tracer, 1)),
            (behind(tracer, 2), beyond(tracer, 2)),
        ]
        tracer = advect(tracer, speeds, neighbours)
    conductivity = archie(porosity, tracer)
    surveys_here = potential_init.shape[0]
    field_shape = potential_init.shape
    electrodes_here = contacts.shape[0]
    global_ids = lax.axis_index("space") * electrodes_here + jnp.arange(
        electrodes_here, dtype=jnp.int32
    )
    contact_cells = contacts.reshape(-1)

    def inject(current):
        spread = jnp.repeat(current / CONTACTS, CONTACTS, axis=1)
        field = (
            jnp.zeros((surveys_here, conductivity.size), jnp.float32)
            .at[:, contact_cells]
            .add(spread)
        )
        return field.reshape(field_shape)

    cond_padded = extended(conductivity, (("space", 0),), 1)
    upper_faces = [
        harmonic(conductivity, cond_padded[2:]),
        harmonic(conductivity, beyond(conductivity, 1)),
        harmonic(conductivity, beyond(conductivity, 2)),
    ]
    lower_faces = [
        harmonic(cond_padded[:-2], conductivity),
        behind(upper_faces[1], 1),
        behind(upper_faces[2], 2),
    ]
    diagonal_sum = (
        upper_faces[0]
        + lower_faces[0]
        + upper_faces[1]
        + lower_faces[1]
        + upper_faces[2]
        + lower_faces[2]
    )

    def relax_sweep(field, source):
        padded = extended(field, (("space", 1),), 1)
        gathered = upper_faces[0] * padded[:, 2:] + lower_faces[0] * padded[:, :-2]
        gathered = gathered + upper_faces[1] * beyond(field, 2) + lower_faces[1] * behind(field, 2)
        gathered = gathered + upper_faces[2] * beyond(field, 3) + lower_faces[2] * behind(field, 3)
        return (1.0 - relaxation) * field + relaxation * (source + gathered) / diagonal_sum

    def solve(field, source):
        for _ in range(RELAX_SWEEPS):
            field = relax_sweep(field, source)
        return field

    current = injected_current * (
        (sources[:, 0:1] == global_ids[None, :]).astype(jnp.float32)
        - (sources[:, 1:2] == global_ids[None, :]).astype(jnp.float32)
    )
    source = inject(current)
    potential = solve(potential_init, source)
    voltage_readings = jnp.sum(potential.reshape(surveys_here, -1)[:, contacts], axis=2) / CONTACTS
    selector = (receivers[:, :, 0:1] == global_ids).astype(jnp.float32) - (
        receivers[:, :, 1:2] == global_ids
    ).astype(jnp.float32)
    all_voltages = lax.all_gather(voltage_readings, "space", axis=1, tiled=True)
    columns = jnp.arange(all_voltages.shape[1], dtype=jnp.int32)
    selector_all = (receivers[:, :, 0:1] == columns).astype(jnp.float32) - (
        receivers[:, :, 1:2] == columns
    ).astype(jnp.float32)
    readings = jnp.einsum("ske,se->sk", selector_all, all_voltages, precision=lax.Precision.HIGHEST)
    misfit = readings - observed
    backward_current = jnp.einsum("sk,ske->se", misfit, selector, precision=lax.Precision.HIGHEST)
    adjoint_source = inject(backward_current)
    adjoint = solve(adjoint_init, adjoint_source)
    next_potential, next_adjoint = passed_along((potential[:, 0], adjoint[:, 0]), "space", -1)
    upper_potential = jnp.concatenate([potential[:, 1:], next_potential[:, None]], axis=1)
    adjoint_up = jnp.concatenate([adjoint[:, 1:], next_adjoint[:, None]], axis=1)
    products = upper_faces[0] * (upper_potential - potential) * (adjoint_up - adjoint)
    products = products + upper_faces[1] * (beyond(potential, 2) - potential) * (
        beyond(adjoint, 2) - adjoint
    )
    products = products + upper_faces[2] * (beyond(potential, 3) - potential) * (
        beyond(adjoint, 3) - adjoint
    )
    local_sum = -jnp.sum(products, axis=0)
    gradient = lax.psum(local_sum, "tm")
    return (gradient, readings)


def solution(mesh):
    return jax.shard_map(
        on_device,
        mesh=mesh,
        in_specs=(
            P("space", None, None),
            P(None, "space", None, None),
            P("space", None, None),
            P("space", None),
            P("tm", None),
            P("tm", None, None),
            P("tm", None),
            P("tm", "space", None, None),
            P("tm", "space", None, None),
        ),
        out_specs=(P("space", None, None), P("tm", None)),
        check_vma=False,
    )
```

profile of v0, /device:TPU:1, one launch (start us, length us, event | category | flops | bytes accessed | tf_op | source)
XLA Modules:
  0.0 877.4 jit_solution(17269980980783226414)
XLA Ops:
  8.1 4.0 collective-permute-start
  12.1 1.3 collective-permute-start.1
  14.4 2.7 collective-permute-done.1
  17.1 1.6 fusion.207
  18.8 3.2 collective-permute-start.2
  22.0 1.3 collective-permute-start.3
  23.3 3.7 collective-permute-done.3
  27.2 4.4 collective-permute-start.4
  31.6 1.3 collective-permute-start.5
  32.9 3.7 collective-permute-done.5
  36.8 4.0 collective-permute-start.6
  40.8 1.3 collective-permute-start.7
  43.1 1.3 collective-permute-start.17
  44.4 4.9 collective-permute-start.19
  49.5 3.8 collective-permute-start.8
  53.3 1.3 collective-permute-start.9
  55.6 2.7 collective-permute-done.9
  58.5 5.7 collective-permute-start.10
  64.2 1.3 collective-permute-start.11
  65.5 3.7 collective-permute-done.11
  69.4 3.7 collective-permute-start.12
  73.2 1.3 collective-permute-start.13
  75.4 2.8 collective-permute-done.13
  78.4 4.0 collective-permute-start.14
  82.4 1.3 collective-permute-start.15
  84.0 7.6 scatter_custom_fusion
  91.6 10.0 %copy.54 = f32[2,2,128,128]{3,2,1,0:T(8,128)S(1)} copy(f32[2,2,128,128]{0,3,2,1:T(8,128)} %bitcast.89) | data formatting | bytes 524288 | tf_op jit(solution)/shard_map/reshape | solution.py:106
  101.9 1.3 collective-permute-start.16
  103.2 5.6 collective-permute-start.18
  110.5 1.3 collective-permute-start.20
  111.8 16.9 %collective-permute-start.21 = (f32[2,1,128,128]{3,2,1,0:T(8,128)S(1)}, f32[2,1,128,128]{3,2,1,0:T(8,128)S(1)}, u32[]{:S(2)}, u32[]{:S(2)}) collective-permute-start(f32[2,1,128,128]{3,2,1,0:T(8,128)S(1)} %get-tuple-element.32), channel_id=1, source_target_pairs={{0,16},{16,32},{32,48},{48,64},{64,80},{80,96},{96,112},{112,128},... | collective-permute-start | bytes 393224 | tf_op jit(solution)/shard_map/ppermute | solution.py:22
  129.2 1.5 collective-permute-done.21
  131.0 1.3 collective-permute-start.22
  132.3 4.4 collective-permute-start.23
  137.1 1.5 collective-permute-done.23
  138.9 1.3 collective-permute-start.24
  140.2 15.2 %collective-permute-start.25 = (f32[2,1,128,128]{3,2,1,0:T(8,128)S(1)}, f32[2,1,128,128]{3,2,1,0:T(8,128)S(1)}, u32[]{:S(2)}, u32[]{:S(2)}) collective-permute-start(f32[2,1,128,128]{3,2,1,0:T(8,128)S(1)} %get-tuple-element.28), channel_id=1, source_target_pairs={{0,16},{16,32},{32,48},{48,64},{64,80},{80,96},{96,112},{112,128},... | collective-permute-start | bytes 393224 | tf_op jit(solution)/shard_map/ppermute | solution.py:22
  155.4 1.3 collective-permute-start.31
  156.7 8.0 collective-permute-start.32
  165.1 1.3 collective-permute-start.26
  166.4 11.5 %collective-permute-start.27 = (f32[2,1,128,128]{3,2,1,0:T(8,128)S(1)}, f32[2,1,128,128]{3,2,1,0:T(8,128)S(1)}, u32[]{:S(2)}, u32[]{:S(2)}) collective-permute-start(f32[2,1,128,128]{3,2,1,0:T(8,128)S(1)} %get-tuple-element.26), channel_id=1, source_target_pairs={{0,16},{16,32},{32,48},{48,64},{64,80},{80,96},{96,112},{112,128},... | collective-permute-start | bytes 393224 | tf_op jit(solution)/shard_map/ppermute | solution.py:22
  178.2 1.5 collective-permute-done.27
  180.0 1.3 collective-permute-start.28
  181.3 6.5 collective-permute-start.29
  188.3 1.5 collective-permute-done.29
  190.0 8.7 copy.61
  198.7 6.4 gather_fusion
  205.2 191.5 %all-gather = f32[32,16,2]{1,2,0:T(2,128)S(1)} all-gather(f32[1,16,2]{1,2,0:T(2,128)S(1)} %bitcast.96), channel_id=1, replica_groups=mesh['space'=32,'tm'=16] {'space'}, dimensions={0}, use_global_device_ids=true | all-gather | bytes 4224 | tf_op jit(solution)/shard_map/all_gather | solution.py:150
  397.7 7.6 scatter_custom_fusion.1
  405.4 10.0 %copy.66 = f32[2,2,128,128]{3,2,1,0:T(8,128)S(1)} copy(f32[2,2,128,128]{0,3,2,1:T(8,128)} %bitcast.88) | data formatting | bytes 524288 | tf_op jit(solution)/shard_map/reshape | solution.py:106
  415.6 1.3 collective-permute-start.33
  416.9 4.0 collective-permute-start.34
  424.4 14.0 %collective-permute-start.36 = (f32[2,1,128,128]{3,2,1,0:T(8,128)S(1)}, f32[2,1,128,128]{3,2,1,0:T(8,128)S(1)}, u32[]{:S(2)}, u32[]{:S(2)}) collective-permute-start(f32[2,1,128,128]{3,2,1,0:T(8,128)S(1)} %get-tuple-element.18), channel_id=1, source_target_pairs={{0,16},{16,32},{32,48},{48,64},{64,80},{80,96},{96,112},{112,128},... | collective-permute-start | bytes 393224 | tf_op jit(solution)/shard_map/ppermute | solution.py:22
  438.9 1.5 collective-permute-done.36
  442.0 4.4 collective-permute-start.38
  446.8 1.5 collective-permute-done.38
  449.9 15.2 %collective-permute-start.40 = (f32[2,1,128,128]{3,2,1,0:T(8,128)S(1)}, f32[2,1,128,128]{3,2,1,0:T(8,128)S(1)}, u32[]{:S(2)}, u32[]{:S(2)}) collective-permute-start(f32[2,1,128,128]{3,2,1,0:T(8,128)S(1)} %get-tuple-element.14), channel_id=1, source_target_pairs={{0,16},{16,32},{32,48},{48,64},{64,80},{80,96},{96,112},{112,128},... | collective-permute-start | bytes 393224 | tf_op jit(solution)/shard_map/ppermute | solution.py:22
  465.6 1.5 collective-permute-done.40
  467.3 1.3 collective-permute-start.41
  468.6 6.5 collective-permute-start.42
  478.7 11.2 %collective-permute-done.30 = f32[2,128,128]{2,1,0:T(8,128)S(1)} collective-permute-done((f32[2,128,128]{2,1,0:T(8,128)S(1)}, f32[2,128,128]{2,1,0:T(8,128)S(1)}, u32[]{:S(2)}, u32[]{:S(2)}) %collective-permute-start.30) | collective-permute-done | bytes 131104 | tf_op jit(solution)/shard_map/ppermute | solution.py:33
  489.9 2.2 collective-permute-done.43
  493.1 375.9 %all-reduce.90.cloned.1.call-done = f32[2,128,128]{2,1,0:T(8,128)} async-done(((f32[2,128,128]{2,1,0:T(8,128)}), f32[2,128,128]{2,1,0:T(8,128)}) %all-reduce.90.cloned.1.call-update) | async-done | bytes 131088 | tf_op jit(solution)/shard_map/psum | solution.py:171
  868.9 1.6 copy.85
  (123 shorter events, 24.9 us)
Async XLA Ops:
  7.2 861.8 %all-reduce.90.cloned.1.call-start = ((), (), s32[]{:S(2)}) async-start(), calls=%async_computation | async-start | bytes 262144 | tf_op jit(solution)/shard_map/psum | solution.py:171
  8.1 6.3 collective-permute-start
  12.1 5.0 collective-permute-start.1
  18.8 4.5 collective-permute-start.2
  22.0 5.0 collective-permute-start.3
  27.2 5.8 collective-permute-start.4
  31.6 5.0 collective-permute-start.5
  36.8 12.5 %collective-permute-start.6 = (f32[1,128,128]{2,1,0:T(8,128)S(1)}, f32[1,128,128]{2,1,0:T(8,128)S(1)}, u32[]{:S(2)}, u32[]{:S(2)}) collective-permute-start(f32[1,128,128]{2,1,0:T(8,128)S(1)} %get-tuple-element.49), channel_id=1, source_target_pairs={{0,16},{16,32},{32,48},{48,64},{64,80},{80,96},{96,112},{112,128},... | collective-permute-start | bytes 196616 | tf_op jit(solution)/shard_map/ppermute | solution.py:22
  40.8 8.5 collective-permute-start.7
  43.1 67.1 %collective-permute-start.17 = (f32[2,1,128,128]{3,2,1,0:T(8,128)S(1)}, f32[2,1,128,128]{3,2,1,0:T(8,128)S(1)}, u32[]{:S(2)}, u32[]{:S(2)}) collective-permute-start(f32[2,1,128,128]{3,2,1,0:T(8,128)S(1)} %get-tuple-element.33), channel_id=1, source_target_pairs={{16,0},{32,16},{48,32},{64,48},{80,64},{96,80},{112,96},{128,112},... | collective-permute-start | bytes 393224 | tf_op jit(solution)/shard_map/ppermute | solution.py:25
  44.4 65.8 %collective-permute-start.19 = (f32[2,1,128,128]{3,2,1,0:T(8,128)S(1)}, f32[2,1,128,128]{3,2,1,0:T(8,128)S(1)}, u32[]{:S(2)}, u32[]{:S(2)}) collective-permute-start(f32[2,1,128,128]{3,2,1,0:T(8,128)S(1)} %get-tuple-element.34), channel_id=1, source_target_pairs={{0,16},{16,32},{32,48},{48,64},{64,80},{80,96},{96,112},{112,128},... | collective-permute-start | bytes 393224 | tf_op jit(solution)/shard_map/ppermute | solution.py:22
  49.5 6.1 collective-permute-start.8
  53.3 5.0 collective-permute-start.9
  58.5 7.0 collective-permute-start.10
  64.2 5.1 collective-permute-start.11
  69.4 6.0 collective-permute-start.12
  73.2 5.0 collective-permute-start.13
  78.4 23.3 %collective-permute-start.14 = (f32[1,128,128]{2,1,0:T(8,128)S(1)}, f32[1,128,128]{2,1,0:T(8,128)S(1)}, u32[]{:S(2)}, u32[]{:S(2)}) collective-permute-start(f32[1,128,128]{2,1,0:T(8,128)S(1)} %get-tuple-element.41), channel_id=1, source_target_pairs={{0,16},{16,32},{32,48},{48,64},{64,80},{80,96},{96,112},{112,128},... | collective-permute-start | bytes 196616 | tf_op jit(solution)/shard_map/ppermute | solution.py:22
  82.4 19.2 %collective-permute-start.15 = (f32[1,128,128]{2,1,0:T(8,128)S(1)}, f32[1,128,128]{2,1,0:T(8,128)S(1)}, u32[]{:S(2)}, u32[]{:S(2)}) collective-permute-start(f32[1,128,128]{2,1,0:T(8,128)S(1)} %get-tuple-element.42), channel_id=1, source_target_pairs={{16,0},{32,16},{48,32},{64,48},{80,64},{96,80},{112,96},{128,112},... | collective-permute-start | bytes 196616 | tf_op jit(solution)/shard_map/ppermute | solution.py:25
  84.0 17.7 %copy-start.2 = (f32[2,128,128]{2,1,0:T(8,128)S(1)}, f32[2,128,128]{2,1,0:T(8,128)}, u32[]{:S(2)}) copy-start(f32[2,128,128]{2,1,0:T(8,128)} %param.11) | copy-start | bytes 393220
  84.0 26.3 %copy-start = (f32[2,2,128,128]{3,2,1,0:T(8,128)S(1)}, f32[2,2,128,128]{3,2,1,0:T(8,128)}, u32[]{:S(2)}) copy-start(f32[2,2,128,128]{3,2,1,0:T(8,128)} %param.16) | copy-start | bytes 786436
  91.6 63.8 %copy-start.1 = (f32[2,2,128,128]{3,2,1,0:T(8,128)S(1)}, f32[2,2,128,128]{3,2,1,0:T(8,128)}, u32[]{:S(2)}) copy-start(f32[2,2,128,128]{3,2,1,0:T(8,128)} %param.17) | copy-start | bytes 786436
  91.6 86.2 %copy-start.3 = (s32[16,4]{0,1:T(4,128)S(1)}, s32[16,4]{0,1:T(4,128)}, u32[]{:S(2)}) copy-start(s32[16,4]{0,1:T(4,128)} %param.12) | copy-start | bytes 772
  91.6 96.2 %copy-start.4 = (s32[2,64,2]{1,2,0:T(2,128)S(1)}, s32[2,64,2]{1,2,0:T(2,128)}, u32[]{:S(2)}) copy-start(s32[2,64,2]{1,2,0:T(2,128)} %param.14) | copy-start | bytes 3076
  101.9 7.0 collective-permute-start.16
  103.2 6.9 collective-permute-start.18
  110.1 287.1 %copy-start.5 = (f32[2,64]{1,0:T(2,128)S(1)}, f32[2,64]{1,0:T(2,128)}, u32[]{:S(2)}) copy-start(f32[2,64]{1,0:T(2,128)} %param.15) | copy-start | bytes 1540
  110.5 18.7 %collective-permute-start.20 = (f32[2,1,128,128]{3,2,1,0:T(8,128)S(1)}, f32[2,1,128,128]{3,2,1,0:T(8,128)S(1)}, u32[]{:S(2)}, u32[]{:S(2)}) collective-permute-start(f32[2,1,128,128]{3,2,1,0:T(8,128)S(1)} %get-tuple-element.31), channel_id=1, source_target_pairs={{16,0},{32,16},{48,32},{64,48},{80,64},{96,80},{112,96},{128,112},... | collective-permute-start | bytes 393224 | tf_op jit(solution)/shard_map/ppermute | solution.py:25
  111.8 18.9 %collective-permute-start.21 = (f32[2,1,128,128]{3,2,1,0:T(8,128)S(1)}, f32[2,1,128,128]{3,2,1,0:T(8,128)S(1)}, u32[]{:S(2)}, u32[]{:S(2)}) collective-permute-start(f32[2,1,128,128]{3,2,1,0:T(8,128)S(1)} %get-tuple-element.32), channel_id=1, source_target_pairs={{0,16},{16,32},{32,48},{48,64},{64,80},{80,96},{96,112},{112,128},... | collective-permute-start | bytes 393224 | tf_op jit(solution)/shard_map/ppermute | solution.py:22
  131.0 6.1 collective-permute-start.22
  132.3 6.3 collective-permute-start.23
  138.9 25.8 %collective-permute-start.24 = (f32[2,1,128,128]{3,2,1,0:T(8,128)S(1)}, f32[2,1,128,128]{3,2,1,0:T(8,128)S(1)}, u32[]{:S(2)}, u32[]{:S(2)}) collective-permute-start(f32[2,1,128,128]{3,2,1,0:T(8,128)S(1)} %get-tuple-element.27), channel_id=1, source_target_pairs={{16,0},{32,16},{48,32},{64,48},{80,64},{96,80},{112,96},{128,112},... | collective-permute-start | bytes 393224 | tf_op jit(solution)/shard_map/ppermute | solution.py:25
  140.2 24.5 %collective-permute-start.25 = (f32[2,1,128,128]{3,2,1,0:T(8,128)S(1)}, f32[2,1,128,128]{3,2,1,0:T(8,128)S(1)}, u32[]{:S(2)}, u32[]{:S(2)}) collective-permute-start(f32[2,1,128,128]{3,2,1,0:T(8,128)S(1)} %get-tuple-element.28), channel_id=1, source_target_pairs={{0,16},{16,32},{32,48},{48,64},{64,80},{80,96},{96,112},{112,128},... | collective-permute-start | bytes 393224 | tf_op jit(solution)/shard_map/ppermute | solution.py:22
  155.4 259.9 %collective-permute-start.31 = (f32[2,1,128,128]{3,2,1,0:T(8,128)S(1)}, f32[2,1,128,128]{3,2,1,0:T(8,128)S(1)}, u32[]{:S(2)}, u32[]{:S(2)}) collective-permute-start(f32[2,1,128,128]{3,2,1,0:T(8,128)S(1)} %get-tuple-element.21), channel_id=1, source_target_pairs={{16,0},{32,16},{48,32},{64,48},{80,64},{96,80},{112,96},{128,112},... | collective-permute-start | bytes 393224 | tf_op jit(solution)/shard_map/ppermute | solution.py:25
  156.7 258.6 %collective-permute-start.32 = (f32[2,1,128,128]{3,2,1,0:T(8,128)S(1)}, f32[2,1,128,128]{3,2,1,0:T(8,128)S(1)}, u32[]{:S(2)}, u32[]{:S(2)}) collective-permute-start(f32[2,1,128,128]{3,2,1,0:T(8,128)S(1)} %get-tuple-element.22), channel_id=1, source_target_pairs={{0,16},{16,32},{32,48},{48,64},{64,80},{80,96},{96,112},{112,128},... | collective-permute-start | bytes 393224 | tf_op jit(solution)/shard_map/ppermute | solution.py:22
  165.1 13.2 %collective-permute-start.26 = (f32[2,1,128,128]{3,2,1,0:T(8,128)S(1)}, f32[2,1,128,128]{3,2,1,0:T(8,128)S(1)}, u32[]{:S(2)}, u32[]{:S(2)}) collective-permute-start(f32[2,1,128,128]{3,2,1,0:T(8,128)S(1)} %get-tuple-element.25), channel_id=1, source_target_pairs={{16,0},{32,16},{48,32},{64,48},{80,64},{96,80},{112,96},{128,112},... | collective-permute-start | bytes 393224 | tf_op jit(solution)/shard_map/ppermute | solution.py:25
  166.4 13.4 %collective-permute-start.27 = (f32[2,1,128,128]{3,2,1,0:T(8,128)S(1)}, f32[2,1,128,128]{3,2,1,0:T(8,128)S(1)}, u32[]{:S(2)}, u32[]{:S(2)}) collective-permute-start(f32[2,1,128,128]{3,2,1,0:T(8,128)S(1)} %get-tuple-element.26), channel_id=1, source_target_pairs={{0,16},{16,32},{32,48},{48,64},{64,80},{80,96},{96,112},{112,128},... | collective-permute-start | bytes 393224 | tf_op jit(solution)/shard_map/ppermute | solution.py:22
  180.0 8.2 collective-permute-start.28
  181.3 8.5 collective-permute-start.29
  397.2 18.2 %copy-start.6 = (f32[2,1,64]{2,1,0:T(1,128)}, f32[2,1,64]{2,1,0:T(1,128)S(1)}, u32[]{:S(2)}) copy-start(f32[2,1,64]{2,1,0:T(1,128)S(1)} %fusion.197) | copy-start | bytes 1540
  415.6 6.0 collective-permute-start.33
  416.9 5.9 collective-permute-start.34
  423.1 15.8 %collective-permute-start.35 = (f32[2,1,128,128]{3,2,1,0:T(8,128)S(1)}, f32[2,1,128,128]{3,2,1,0:T(8,128)S(1)}, u32[]{:S(2)}, u32[]{:S(2)}) collective-permute-start(f32[2,1,128,128]{3,2,1,0:T(8,128)S(1)} %get-tuple-element.17), channel_id=1, source_target_pairs={{16,0},{32,16},{48,32},{64,48},{80,64},{96,80},{112,96},{128,112},... | collective-permute-start | bytes 393224 | tf_op jit(solution)/shard_map/ppermute | solution.py:25
  424.4 16.0 %collective-permute-start.36 = (f32[2,1,128,128]{3,2,1,0:T(8,128)S(1)}, f32[2,1,128,128]{3,2,1,0:T(8,128)S(1)}, u32[]{:S(2)}, u32[]{:S(2)}) collective-permute-start(f32[2,1,128,128]{3,2,1,0:T(8,128)S(1)} %get-tuple-element.18), channel_id=1, source_target_pairs={{0,16},{16,32},{32,48},{48,64},{64,80},{80,96},{96,112},{112,128},... | collective-permute-start | bytes 393224 | tf_op jit(solution)/shard_map/ppermute | solution.py:22
  440.7 6.1 collective-permute-start.37
  442.0 6.3 collective-permute-start.38
  448.6 17.0 %collective-permute-start.39 = (f32[2,1,128,128]{3,2,1,0:T(8,128)S(1)}, f32[2,1,128,128]{3,2,1,0:T(8,128)S(1)}, u32[]{:S(2)}, u32[]{:S(2)}) collective-permute-start(f32[2,1,128,128]{3,2,1,0:T(8,128)S(1)} %get-tuple-element.13), channel_id=1, source_target_pairs={{16,0},{32,16},{48,32},{64,48},{80,64},{96,80},{112,96},{128,112},... | collective-permute-start | bytes 393224 | tf_op jit(solution)/shard_map/ppermute | solution.py:25
  449.9 17.2 %collective-permute-start.40 = (f32[2,1,128,128]{3,2,1,0:T(8,128)S(1)}, f32[2,1,128,128]{3,2,1,0:T(8,128)S(1)}, u32[]{:S(2)}, u32[]{:S(2)}) collective-permute-start(f32[2,1,128,128]{3,2,1,0:T(8,128)S(1)} %get-tuple-element.14), channel_id=1, source_target_pairs={{0,16},{16,32},{32,48},{48,64},{64,80},{80,96},{96,112},{112,128},... | collective-permute-start | bytes 393224 | tf_op jit(solution)/shard_map/ppermute | solution.py:22
  467.3 9.2 %collective-permute-start.41 = (f32[2,1,128,128]{3,2,1,0:T(8,128)S(1)}, f32[2,1,128,128]{3,2,1,0:T(8,128)S(1)}, u32[]{:S(2)}, u32[]{:S(2)}) collective-permute-start(f32[2,1,128,128]{3,2,1,0:T(8,128)S(1)} %get-tuple-element.11), channel_id=1, source_target_pairs={{16,0},{32,16},{48,32},{64,48},{80,64},{96,80},{112,96},{128,112},... | collective-permute-start | bytes 393224 | tf_op jit(solution)/shard_map/ppermute | solution.py:25
  468.6 8.5 collective-permute-start.42
  475.2 14.7 %collective-permute-start.30 = (f32[2,128,128]{2,1,0:T(8,128)S(1)}, f32[2,128,128]{2,1,0:T(8,128)S(1)}, u32[]{:S(2)}, u32[]{:S(2)}) collective-permute-start(f32[2,128,128]{2,1,0:T(8,128)S(1)} %get-tuple-element.10), channel_id=1, source_target_pairs={{16,0},{32,16},{48,32},{64,48},{80,64},{96,80},{112,96},{128,112},... | collective-permute-start | bytes 393224 | tf_op jit(solution)/shard_map/ppermute | solution.py:33
  477.4 14.7 %collective-permute-start.43 = (f32[2,128,128]{2,1,0:T(8,128)S(1)}, f32[2,128,128]{2,1,0:T(8,128)S(1)}, u32[]{:S(2)}, u32[]{:S(2)}) collective-permute-start(f32[2,128,128]{2,1,0:T(8,128)S(1)} %get-tuple-element.8), channel_id=1, source_target_pairs={{16,0},{32,16},{48,32},{64,48},{80,64},{96,80},{112,96},{128,112},... | collective-permute-start | bytes 393224 | tf_op jit(solution)/shard_map/ppermute | solution.py:33
Sparse Core Ops, SparseCore 0:
  493.2 375.7 all-reduce.89
where the time goes:
time: 879 us; the launch traced here: 877 us
  waiting for transfers between devices  426 us (48%)
  blocking collectives  191 us (22%)
  starting transfers between devices  180 us (20%)
  local copies, waits for them, and re-layouts  41.5 us (5%)
  other arithmetic  23.2 us (3%)
  between operations  14.9 us (2%)
    psum x1, waiting for transfers between devices, on_device(): gradient = lax.psum(local_sum, 'tm')  376 us
    all_gather x1, blocking collectives, on_device(): all_voltages = lax.all_gather(voltage_readings, 'space', axis=1, tiled=True)  191 us
    ppermute x21, starting transfers between devices, extended(): lax.ppermute(lax.slice_in_dim(block, block.shape[dim] - width, None, axis...  150 us
    ppermute x21, starting transfers between devices, extended(): lax.ppermute(lax.slice_in_dim(block, 0, width, axis=dim), axis, backward)  27.1 us
    ppermute x21, waiting for transfers between devices, extended(): lax.ppermute(lax.slice_in_dim(block, 0, width, axis=dim), axis, backward)  22.8 us
    reshape x2, local copies, waits for them, and re-layouts, inject(): return field.reshape(field_shape)  20 us
  transfers between devices with their start and end apart: 45, of which 27 were waited for; matrix products, arithmetic and copies ran while one was open for 7% of the time, Pallas kernels for 0%

commit v1 on v0

v1 whole, which is shorter than its diff:
```python
import jax
import jax.numpy as jnp
from jax import lax
from jax.experimental import pallas as pl
from jax.experimental.pallas import tpu as pltpu
from jax.sharding import PartitionSpec as P

STEPS = 8
RELAX_SWEEPS = 6
MESH = pl.DeviceIdType.MESH
HIGH = lax.Precision.HIGHEST
F32 = jnp.float32


def harmonic(first, second):
    return 2.0 * (first * second) / (first + second)


def iota(shape, dim):
    return lax.broadcasted_iota(jnp.int32, shape, dim)


def dot(a, b):
    return lax.dot_general(a, b, (((1,), (0,)), ((), ())), precision=HIGH, preferred_element_type=F32)


def dot_t(a, b):
    return lax.dot_general(a, b, (((1,), (1,)), ((), ())), precision=HIGH, preferred_element_type=F32)


def kernel(
    inp, pot, adj, meta, grad, read,
    ct, yct, yst, tv, sg, ysg, yss, coef, rdiag, bsrc,
    pf, ypf, ypsend, af, yaf, yasend,
    mbuf, rt, lt, vb, vsend, vall, rsend, rdin,
    gbuf, grx, gsum, rsbuf, osum,
    in_s, in_r, rel_s, t_s, t_r, sw_s, sw_r, sg_s, sg_r, tile_s, tile_r,
    p_s, p_r, a_s, a_r, v_s, v_r, rd_s, rd_r, gx_s, gx_r, rs_s, rs_r, ag_s, ag_r,
):
    space = lax.axis_index("space")
    tm = lax.axis_index("tm")
    zh = space // 16
    x = (space // 4) % 4
    y = space % 4
    zl = tm // 2
    c = tm % 2
    z = zh * 8 + zl

    def dev(x_, y_, z_, c_):
        return {"space": (z_ // 8) * 16 + x_ * 4 + y_, "tm": (z_ % 8) * 2 + c_}

    def remote(src, dst, s, r, where):
        return pltpu.make_async_remote_copy(
            src_ref=src, dst_ref=dst, send_sem=s, recv_sem=r, device_id=where, device_id_type=MESH
        )

    def arrived(ref, sem):
        pltpu.make_async_copy(ref, ref, sem).wait()

    xn = (x + 1) % 4
    xp = (x + 3) % 4
    yn = (y + 1) % 4
    yp = (y + 3) % 4
    x_last = (x + 1) // 4
    x_first = (3 - x) // 3
    y_last = (y + 1) // 4
    y_first = (3 - y) // 3

    zero_plane = jnp.zeros((32, 128), F32)

    @pl.when((x == 0) & (c == 0))
    def _():
        for par in range(2):
            ct[par, 0] = zero_plane

    @pl.when((x == 3) & (c == 1))
    def _():
        for par in range(2):
            ct[par, 9] = zero_plane

    @pl.when(x == 0)
    def _():
        sg[1, 0] = zero_plane
        for f in (pf, af):
            for par in range(2):
                f[par, 1, 0] = zero_plane

    @pl.when(x == 3)
    def _():
        sg[2, 9] = zero_plane
        for f in (pf, af):
            for par in range(2):
                f[par, 2, 9] = zero_plane

    for d in range(2):
        @pl.when(y == 3 * d)
        def _():
            ysg[d, 0] = jnp.zeros((2, 8, 128), F32)
            for par in range(2):
                yct[par, d, 0] = jnp.zeros((8, 128), F32)

    zz = (z + 8 * c) % 16
    home = zz < 8

    def landing(a):
        return ct.at[0, pl.ds(1, 8)] if a == 0 else tv.at[a - 1]

    def landing_two(a):
        return ct.at[0, pl.ds(1 + 2 * y, 2)] if a == 0 else tv.at[a - 1, pl.ds(2 * y, 2)]

    def in_copy(a, d):
        yt = (y + d) % 4
        rows = pl.ds(pl.multiple_of(32 * yt, 32), 32)
        return remote(inp.at[a, :, rows], landing_two(a), in_s.at[a, d], in_r.at[a], dev(x, yt, z, c))

    def in_local(a):
        rows = pl.ds(pl.multiple_of(32 * y, 32), 32)
        return pltpu.make_async_copy(inp.at[a, :, rows], landing_two(a), in_r.at[a])

    @pl.when(home)
    def _():
        for a in range(5):
            for d in range(1, 4):
                in_copy(a, d).start()
            in_local(a).start()

    up = jnp.where((zz >= 7) & (zz <= 10), 1, 0)
    down = jnp.where((zz == 0) | (zz >= 13), 1, 0)
    zt = (z + up + 15 * down) % 16

    def relay(a):
        return remote(landing(a), landing(a), rel_s.at[a], in_r.at[a], dev(x, y, zt, c))

    for a in range(5):
        arrived(landing(a), in_r.at[a])

        @pl.when(up + down > 0)
        def _():
            relay(a).start()

    def swap_copies(which, j):
        up4 = (j + zh + 1) % 2
        zt4 = (z + 4 * up4 + 12 * (1 - up4)) % 16
        copies = []
        for yt in range(4):
            where = dev(x, yt, zt4, c)
            if which == 2:
                copies.append(remote(meta.at[j], mbuf.at[zh * 4 + y], sw_s.at[2, j, yt], sw_r.at[2], where))
            else:
                src = (pot, adj)[which].at[j, :, pl.ds(32 * yt, 32)]
                dst = (pf, af)[which].at[0, 1 + zh, pl.ds(1 + 2 * y, 2)]
                copies.append(remote(src, dst, sw_s.at[which, j, yt], sw_r.at[which], where))
        return copies

    for which in (2, 0, 1):
        for j in range(2):
            for copy in swap_copies(which, j):
                copy.start()

    @pl.when(up + down > 0)
    def _():
        for a in range(5):
            relay(a).wait_send()

    def t_copies(par):
        return [
            remote(ct.at[par, 8], ct.at[par, 10 * x_last * c], t_s.at[par, 0], t_r.at[par, 0],
                   dev(xn, y, z, (c + x_last) % 2)),
            remote(ct.at[par, 1], ct.at[par, 9 + 2 * x_first * (1 - c)], t_s.at[par, 1], t_r.at[par, 1],
                   dev(xp, y, z, (c + x_first) % 2)),
            remote(yst.at[par, 0], yct.at[par, 0, y_last], t_s.at[par, 2], t_r.at[par, 2], dev(x, yn, z, c)),
            remote(yst.at[par, 1], yct.at[par, 1, y_first], t_s.at[par, 3], t_r.at[par, 3], dev(x, yp, z, c)),
        ]

    row = iota((32, 128), 0)
    lane = iota((32, 128), 1)

    def shift_y(v, low, high):
        below = jnp.where(row == 0, low, pltpu.roll(v, 1, 0))
        above = jnp.where(row == 31, high, pltpu.roll(v, 31, 0))
        return below, above

    def t_rows(par, p, v):
        yst[par, 0, pl.ds(p, 1), :] = v[31:32]
        yst[par, 1, pl.ds(p, 1), :] = v[0:1]

    def first_rows(p, carry):
        t_rows(0, p, ct[0, p + 1])
        return carry

    lax.fori_loop(0, 8, first_rows, 0)
    for copy in t_copies(0):
        copy.start()

    def t_step(s, carry):
        par = s % 2
        new = 1 - par
        for copy in t_copies(par):
            copy.wait()

        def plane(p, inner):
            v = ct[par, p + 1]
            xlow = ct[par, p]
            xhigh = ct[par, p + 2]
            ylow, yhigh = shift_y(v, yct[par, 0, 0, pl.ds(p, 1), :], yct[par, 1, 0, pl.ds(p, 1), :])
            zlow = jnp.where(lane == 0, 0.0, pltpu.roll(v, 1, 1))
            zhigh = jnp.where(lane == 127, 0.0, pltpu.roll(v, 127, 1))
            change = jnp.zeros((32, 128), F32)
            for d, (low, high) in enumerate(((xlow, xhigh), (ylow, yhigh), (zlow, zhigh))):
                speed = tv[d, p]
                change = change + jnp.maximum(speed, 0.0) * (v - low) + jnp.minimum(speed, 0.0) * (high - v)
            v = v - change
            ct[new, p + 1] = v
            t_rows(new, p, v)
            return inner

        lax.fori_loop(0, 8, plane, 0)

        @pl.when(s < STEPS - 1)
        def _():
            for copy in t_copies(new):
                copy.start()

        return carry

    lax.fori_loop(0, STEPS, t_step, 0)

    def conduct(p, carry):
        v = jnp.exp(1.8 * jnp.log(tv[3, p])) * (0.5 + ct[0, p + 1])
        sg[1 + c, p + 1] = v
        yss[0, pl.ds(p, 1), :] = v[31:32]
        yss[1, pl.ds(p, 1), :] = v[0:1]
        return carry

    lax.fori_loop(0, 8, conduct, 0)

    def sg_copies():
        copies = []
        for cc in range(2):
            copies += [
                remote(sg.at[1 + c, 8], sg.at[1 + c + x_last, 0], sg_s.at[0, cc], sg_r.at[0, c], dev(xn, y, z, cc)),
                remote(sg.at[1 + c, 1], sg.at[1 + c - x_first, 9], sg_s.at[1, cc], sg_r.at[1, c], dev(xp, y, z, cc)),
                remote(yss.at[0], ysg.at[0, y_last, c], sg_s.at[2, cc], sg_r.at[2, c], dev(x, yn, z, cc)),
                remote(yss.at[1], ysg.at[1, y_first, c], sg_s.at[3, cc], sg_r.at[3, c], dev(x, yp, z, cc)),
            ]
        return copies

    tile_copy = remote(
        sg.at[1 + c, pl.ds(1, 8)], sg.at[1 + c, pl.ds(1, 8)], tile_s, tile_r, dev(x, y, z, 1 - c)
    )
    tile_copy.start()
    for copy in sg_copies():
        copy.start()

    arrived(mbuf, sw_r.at[2])

    def tables(k, carry):
        q = iota((64, 128), 0)
        target = ((q // 32) * 128 + q % 32 + 32 * y).astype(F32)
        rt[k] = jnp.where(target == mbuf[k, 0:1, :], 1.0, 0.0)
        lt[k] = jnp.where(iota((128, 128), 0).astype(F32) == mbuf[k, 1:2, :], 1.0, 0.0)
        return carry

    lax.fori_loop(0, 8, tables, 0)
    jj = iota((128, 128), 0)
    mm = iota((128, 128), 1)
    spread = jnp.where((jj % 16 == mm % 16) & (mm < 64), 0.25, 0.0)
    own = jnp.where(iota((8, 128), 1) // 16 == iota((8, 128), 0), 1.0, 0.0)
    r0 = mbuf[0, 2:3, :]
    r1 = mbuf[0, 3:4, :]
    observed = mbuf[0, 4:5, :]
    ja = mbuf[0, 5:6, :]
    jb = mbuf[0, 6:7, :]

    tile_copy.wait()
    for copy in sg_copies():
        copy.wait_send()
    for d in range(4):
        for cc in range(2):
            if d < 2:
                arrived(sg.at[1, 0], sg_r.at[d, cc])
            else:
                arrived(yss.at[0], sg_r.at[d, cc])

    def faces_of(h, p):
        s = sg[1 + h, p + 1]
        low = ysg[0, 0, h, pl.ds(p, 1), :]
        high = ysg[1, 0, h, pl.ds(p, 1), :]
        _, syp = shift_y(s, low, high)
        szp = jnp.where(lane == 127, 0.0, pltpu.roll(s, 127, 1))
        ux = harmonic(s, sg[1 + h, p + 2])
        uy = harmonic(s, syp)
        uz = harmonic(s, szp)
        return s, low, ux, uy, uz

    def coefficients(h):
        def plane(p, lx):
            s, low, ux, uy, uz = faces_of(h, p)
            ly = jnp.where(row == 0, harmonic(low, s[0:1]), pltpu.roll(uy, 1, 0))
            lz = pltpu.roll(uz, 1, 1)
            r = 0.8 / (ux + lx + uy + ly + uz + lz)
            rdiag[h, p] = r
            for k, face in enumerate((ux, lx, uy, ly, uz, lz)):
                coef[k, h, p] = face * r
            return ux

        lax.fori_loop(0, 8, plane, harmonic(sg[1 + h, 0], sg[1 + h, 1]))

    for h in range(2):
        coefficients(h)

    def inject(current):
        vals = dot(jnp.broadcast_to(current, (8, 128)) * own, spread)
        for k in range(8):
            h, pair = k // 4, 2 * (k % 4)
            block = dot_t(rt[k], lt[k] * vals[k : k + 1, :])
            bsrc[h, pair] = block[0:32] * rdiag[h, pair]
            bsrc[h, pair + 1] = block[32:64] * rdiag[h, pair + 1]

    def field(f, yf, ysend, s_sem, r_sem):
        def copies(par):
            return [
                remote(f.at[par, pl.ds(1, 2), 8], f.at[par, pl.ds(1 + x_last, 2), 0],
                       s_sem.at[par, 0], r_sem.at[par, 0], dev(xn, y, z, c)),
                remote(f.at[par, pl.ds(1, 2), 1], f.at[par, pl.ds(1 - x_first, 2), 9],
                       s_sem.at[par, 1], r_sem.at[par, 1], dev(xp, y, z, c)),
                remote(ysend.at[par, 0], yf.at[par, 0], s_sem.at[par, 2], r_sem.at[par, 2], dev(x, yn, z, c)),
                remote(ysend.at[par, 1], yf.at[par, 1], s_sem.at[par, 3], r_sem.at[par, 3], dev(x, yp, z, c)),
            ]

        def edge_rows(par, h, p, v):
            ysend[par, 0, h, pl.ds(p, 1), :] = v[31:32]
            ysend[par, 1, h, pl.ds(p, 1), :] = v[0:1]

        def begin():
            for h in range(2):
                def plane(p, carry):
                    edge_rows(0, h, p, f[0, 1 + h, p + 1])
                    return carry

                lax.fori_loop(0, 8, plane, 0)
            for copy in copies(0):
                copy.start()

        def sweep(s, carry):
            par = s % 2
            new = 1 - par
            for copy in copies(par):
                copy.wait()
            for h in range(2):
                def plane(p, inner):
                    v = f[par, 1 + h, p + 1]
                    ylow, yhigh = shift_y(v, yf[par, 0, h, pl.ds(p, 1), :], yf[par, 1, h, pl.ds(p, 1), :])
                    out = coef[0, h, p] * f[par, 1 + h, p + 2] + coef[1, h, p] * f[par, 1 + h, p]
                    out = out + (coef[2, h, p] * yhigh + coef[3, h, p] * ylow)
                    out = out + (coef[4, h, p] * pltpu.roll(v, 127, 1) + coef[5, h, p] * pltpu.roll(v, 1, 1))
                    out = (0.2 * v + bsrc[h, p]) + out
                    f[new, 1 + h, p + 1] = out
                    edge_rows(new, h, p, out)
                    return inner

                lax.fori_loop(0, 8, plane, 0)
            for copy in copies(new):
                copy.start()
            return carry

        def sweeps():
            lax.fori_loop(0, RELAX_SWEEPS, sweep, 0)

        def end():
            for copy in copies(0):
                copy.wait()

        return begin, sweeps, end

    def electrode_ids(x_):
        j = iota((128, 128), 0)
        return ((j // 64) * 256 + x_ * 64 + j % 64).astype(F32)

    own_lane = iota((1, 128), 1)
    own_ids = ((own_lane // 64) * 256 + x * 64 + own_lane % 64).astype(F32)
    inject(4.0 * (jnp.where(own_ids == ja, 1.0, 0.0) - jnp.where(own_ids == jb, 1.0, 0.0)))

    p_begin, p_sweeps, p_end = field(pf, ypf, ypsend, p_s, p_r)
    a_begin, a_sweeps, a_end = field(af, yaf, yasend, a_s, a_r)
    arrived(pf.at[0, pl.ds(1, 2), pl.ds(1, 8)], sw_r.at[0])
    p_begin()
    p_sweeps()

    for k in range(8):
        h, pair = k // 4, 2 * (k % 4)
        block = pf[0, 1 + h, pl.ds(1 + pair, 2)].reshape(64, 128)
        vb[k : k + 1, :] = jnp.sum(rt[k] * dot(block, lt[k]), axis=0, keepdims=True)
    part = jnp.sum(dot_t(vb[...], spread) * own, axis=0, keepdims=True)
    vsend[...] = jnp.broadcast_to(part, (8, 128))

    def v_copy(k):
        xt = (x + k // 4) % 4
        yt = (y + k % 4) % 4
        return remote(vsend, vall.at[x * 4 + y], v_s.at[k], v_r, dev(xt, yt, z, c))

    for k in range(1, 16):
        v_copy(k).start()
    pltpu.make_async_copy(vsend, vall.at[x * 4 + y], v_r).start()
    arrived(af.at[0, pl.ds(1, 2), pl.ds(1, 8)], sw_r.at[1])
    a_begin()
    arrived(vall, v_r)

    def selector(x_):
        ids = electrode_ids(x_)
        return jnp.where(ids == r0, 1.0, 0.0) - jnp.where(ids == r1, 1.0, 0.0)

    readings = jnp.zeros((8, 128), F32)
    for k in range(4):
        volts = vall[4 * k] + vall[4 * k + 1] + vall[4 * k + 2] + vall[4 * k + 3]
        readings = readings + dot(volts, selector(k))
    rsend[...] = readings
    survey = (1 + zh + zl // 4) % 2

    def read_copies():
        return [
            remote(rsend, rdin.at[survey], rd_s.at[half], rd_r, dev(x, y, half * 8 + (zl + 4) % 8, c))
            for half in range(2)
        ]

    for copy in read_copies():
        copy.start()
    inject(dot_t(readings - observed, selector(x))[0:1])
    a_sweeps()
    p_end()
    a_end()

    for h in range(2):
        def terms(p, carry):
            _, _, ux, uy, uz = faces_of(h, p)
            pv = pf[0, 1 + h, p + 1]
            av = af[0, 1 + h, p + 1]
            _, py = shift_y(pv, pv[0:1], ypf[0, 1, h, pl.ds(p, 1), :])
            _, ay = shift_y(av, av[0:1], yaf[0, 1, h, pl.ds(p, 1), :])
            out = ux * (pf[0, 1 + h, p + 2] - pv) * (af[0, 1 + h, p + 2] - av)
            out = out + uy * (py - pv) * (ay - av)
            out = out + uz * (pltpu.roll(pv, 127, 1) - pv) * (pltpu.roll(av, 127, 1) - av)
            gbuf[h, p] = -out
            return carry

        lax.fori_loop(0, 8, terms, 0)

    other = remote(gbuf.at[1 - c], grx, gx_s, gx_r, dev(x, y, z, 1 - c))
    other.start()
    other.wait()

    def pair_sum(p, carry):
        gsum[p] = gbuf[c, p] + grx[p]
        return carry

    lax.fori_loop(0, 8, pair_sum, 0)

    def rs_copy(k, local):
        p, rh = k // 2, k % 2
        src = gsum.at[p, pl.ds(16 * rh, 16)]
        dst = rsbuf.at[z]
        if local:
            return pltpu.make_async_copy(src, dst, rs_r)
        return remote(src, dst, rs_s.at[k], rs_r, dev(x, y, 8 * c + p, rh))

    def rs_self(k):
        return (z == 8 * c + k // 2) & (c == k % 2)

    for k in range(16):
        @pl.when(jnp.logical_not(rs_self(k)))
        def _():
            rs_copy(k, False).start()

        @pl.when(rs_self(k))
        def _():
            rs_copy(k, True).start()

    arrived(rsbuf, rs_r)
    total = rsbuf[0]
    for k in range(1, 16):
        total = total + rsbuf[k]
    osum[...] = total

    def ag_copy(k, local):
        dst = grad.at[zl % 2, pl.ds(pl.multiple_of(32 * y + 16 * c, 16), 16)]
        if local:
            return pltpu.make_async_copy(osum, dst, ag_r)
        return remote(osum, dst, ag_s.at[k], ag_r, dev(x, zl // 2, 8 * zh + k // 2, k % 2))

    def ag_self(k):
        return (y == zl // 2) & (zl == k // 2) & (c == k % 2)

    for k in range(16):
        @pl.when(jnp.logical_not(ag_self(k)))
        def _():
            ag_copy(k, False).start()

        @pl.when(ag_self(k))
        def _():
            ag_copy(k, True).start()

    arrived(rdin, rd_r)
    read[0:1, :] = rdin[0, 0:1, :]
    read[1:2, :] = rdin[1, 0:1, :]
    arrived(grad, ag_r)

    @pl.when(home)
    def _():
        for a in range(5):
            for d in range(1, 4):
                in_copy(a, d).wait_send()

    for which in range(3):
        for j in range(2):
            for copy in swap_copies(which, j):
                copy.wait_send()
    for k in range(1, 16):
        v_copy(k).wait_send()
    for copy in read_copies():
        copy.wait_send()
    for k in range(16):
        @pl.when(jnp.logical_not(rs_self(k)))
        def _():
            rs_copy(k, False).wait_send()

        @pl.when(jnp.logical_not(ag_self(k)))
        def _():
            ag_copy(k, False).wait_send()


def on_device(
    concentration, velocity, porosity, contacts, sources, receivers, observed, potential_init, adjoint_init
):
    inp = jnp.concatenate([concentration[None], velocity.astype(F32), porosity[None]], axis=0)
    cells = contacts.T.reshape(1, 64)
    pad = jnp.full((1, 64), -1, jnp.int32)
    where = jnp.concatenate([cells // 128, pad], axis=1).astype(F32)
    lanes = jnp.concatenate([cells % 128, pad], axis=1).astype(F32)
    gap = jnp.full((2, 64), -1.0, F32)
    meta = jnp.stack(
        [
            jnp.broadcast_to(where, (2, 128)),
            jnp.broadcast_to(lanes, (2, 128)),
            jnp.concatenate([receivers[:, :, 0].astype(F32), gap], axis=1),
            jnp.concatenate([receivers[:, :, 1].astype(F32), gap], axis=1),
            jnp.concatenate([observed, jnp.zeros((2, 64), F32)], axis=1),
            jnp.broadcast_to(sources[:, 0:1].astype(F32), (2, 128)),
            jnp.broadcast_to(sources[:, 1:2].astype(F32), (2, 128)),
            jnp.zeros((2, 128), F32),
        ],
        axis=1,
    )
    V = pltpu.VMEM
    D = pltpu.SemaphoreType.DMA
    scratch = [
        V((2, 12, 32, 128), F32), V((2, 2, 2, 8, 128), F32), V((2, 2, 8, 128), F32), V((4, 8, 32, 128), F32),
        V((4, 10, 32, 128), F32), V((2, 2, 2, 8, 128), F32), V((2, 8, 128), F32),
        V((6, 2, 8, 32, 128), F32), V((2, 8, 32, 128), F32), V((2, 8, 32, 128), F32),
        V((2, 4, 10, 32, 128), F32), V((2, 2, 2, 8, 128), F32), V((2, 2, 2, 8, 128), F32),
        V((2, 4, 10, 32, 128), F32), V((2, 2, 2, 8, 128), F32), V((2, 2, 2, 8, 128), F32),
        V((8, 8, 128), F32), V((8, 64, 128), F32), V((8, 128, 128), F32), V((8, 128), F32), V((8, 128), F32),
        V((16, 8, 128), F32), V((8, 128), F32), V((2, 8, 128), F32),
        V((2, 8, 32, 128), F32), V((8, 32, 128), F32), V((8, 32, 128), F32), V((16, 16, 128), F32), V((16, 128), F32),
        D((5, 4)), D((5,)), D((5,)), D((2, 4)), D((2, 4)), D((3, 2, 4)), D((3,)), D((4, 2)), D((4, 2)), D, D,
        D((2, 4)), D((2, 4)), D((2, 4)), D((2, 4)), D((16,)), D, D((2,)), D, D, D, D((16,)), D, D((16,)), D,
    ]
    gradient, readings = pl.pallas_call(
        kernel,
        out_shape=(jax.ShapeDtypeStruct((2, 128, 128), F32), jax.ShapeDtypeStruct((2, 128), F32)),
        in_specs=[pl.BlockSpec(memory_space=pl.ANY)] * 4,
        out_specs=(pl.BlockSpec(memory_space=pltpu.VMEM), pl.BlockSpec(memory_space=pltpu.VMEM)),
        scratch_shapes=scratch,
        compiler_params=pltpu.CompilerParams(has_side_effects=True),
        name="survey_gradient",
    )(inp, potential_init, adjoint_init, meta)
    return gradient, readings[:, :64]


def solution(mesh):
    return jax.shard_map(
        on_device,
        mesh=mesh,
        in_specs=(
            P("space", None, None),
            P(None, "space", None, None),
            P("space", None, None),
            P("space", None),
            P("tm", None),
            P("tm", None, None),
            P("tm", None),
            P("tm", "space", None, None),
            P("tm", "space", None, None),
        ),
        out_specs=(P("space", None, None), P("tm", None)),
        check_vma=False,
    )
```

time: 879 us -> 208 us (0.24)
  the two profiles are of different devices: /device:TPU:1 before, /device:TPU:17 now
where the time goes in v1:
time: 208 us; the launch traced here: 207 us
  Pallas kernels  199 us (96%)
  local copies, waits for them, and re-layouts  5.07 us (2%)
  other arithmetic  2.09 us (1%)
    pallas_call x1, Pallas kernels, on_device(): pl.pallas_call(kernel, out_shape=(jax.ShapeDtypeStruct((2, 128, 128), F32...  199 us
    unnamed x16, local copies, waits for them, and re-layouts  4.2 us

profile of v1, /device:TPU:17, one launch (start us, length us, event | category | flops | bytes accessed | tf_op | source)
XLA Modules:
  0.0 207.3 jit_solution(5596926127077130134)
XLA Ops:
  0.6 0.0 copy-start
  0.6 0.0 copy-start.1
  0.6 1.0 convert_element_type.35
  1.7 0.0 copy-done
  1.7 0.0 copy-done.1
  1.7 0.0 copy-start.3
  1.7 0.9 pad_maximum_fusion.inp
  2.6 0.0 copy-done.3
  2.6 0.1 reshape.161
  2.7 0.0 copy-start.4
  2.7 0.7 copy-done.4
  3.4 0.0 copy-start.5
  3.4 0.7 copy-done.5
  4.1 0.0 copy-start.2
  4.1 0.7 copy-done.2
  4.8 0.2 convert_reduce_fusion
  5.0 0.1 stack_broadcast_in_dim.12
  5.0 0.1 stack_broadcast_in_dim.26
  5.1 0.6 stack.15.meta
  5.7 199.5 %survey_gradient.1 = (f32[2,128,128]{2,1,0:T(8,128)}, f32[2,128]{1,0:T(2,128)}) custom-call(f32[5,2,128,128]{3,2,1,0:T(8,128)} %pad_maximum_fusion.inp, f32[2,2,128,128]{3,2,1,0:T(8,128)} %pot.1, f32[2,2,128,128]{3,2,1,0:T(8,128)} %adj.1, f32[2,8,128]{2,1,0:T(8,128)} %stack.15.meta), custom_call_target="tpu_custom_call" | custom-call | tf_op jit(solution)/shard_map/survey_gradient/pallas_call | solution.py:567
  205.2 0.0 copy-start.6
  205.2 1.6 copy.13
  206.8 0.0 copy-done.6
  206.8 0.6 copy.14
  (9 shorter events, 0.1 us)
Async XLA Ops:
  0.6 1.0 copy-start
  0.6 1.1 copy-start.1
  1.7 0.9 copy-start.3
  2.7 0.7 copy-start.4
  3.4 0.7 copy-start.5
  4.1 0.7 copy-start.2
  205.2 1.6 copy-start.6

commit v2 on v1

--- a/solution.py
+++ b/solution.py
@@ -57,14 +57,32 @@
     def arrived(ref, sem):
         pltpu.make_async_copy(ref, ref, sem).wait()
 
+    def start_y(copies):
+        @pl.when(y < 3)
+        def _():
+            copies[0].start()
+
+        @pl.when(y > 0)
+        def _():
+            copies[1].start()
+
+    def wait_y(copies):
+        @pl.when(y < 3)
+        def _():
+            copies[0].wait_send()
+            copies[1].wait_recv()
+
+        @pl.when(y > 0)
+        def _():
+            copies[1].wait_send()
+            copies[0].wait_recv()
+
     xn = (x + 1) % 4
     xp = (x + 3) % 4
     yn = (y + 1) % 4
     yp = (y + 3) % 4
     x_last = (x + 1) // 4
     x_first = (3 - x) // 3
-    y_last = (y + 1) // 4
-    y_first = (3 - y) // 3
 
     zero_plane = jnp.zeros((32, 128), F32)
 
@@ -96,8 +114,38 @@
         @pl.when(y == 3 * d)
         def _():
             ysg[d, 0] = jnp.zeros((2, 8, 128), F32)
+            for yf in (ypf, yaf):
+                for par in range(2):
+                    yf[par, d] = jnp.zeros((2, 8, 128), F32)
             for par in range(2):
                 yct[par, d, 0] = jnp.zeros((8, 128), F32)
+
+    barrier = pltpu.get_barrier_semaphore()
+
+    def greet(where):
+        pl.semaphore_signal(barrier, inc=1, device_id=where, device_id_type=MESH)
+
+    def greet_half(k, carry):
+        greet(dev(x, (y + k // 16) % 4, 8 * zh + (zl + (k // 2) % 8) % 8, (c + k % 2) % 2))
+        return carry
+
+    def greet_column(k, carry):
+        greet(dev(x, y, 8 * (1 - zh) + k // 2, k % 2))
+        return carry
+
+    def greet_far(k, carry):
+        greet(dev(x, (y + k) % 4, (z + 4 * (zl // 4) + 12 * (1 - zl // 4)) % 16, c))
+        return carry
+
+    def greet_plane(k, carry):
+        greet(dev((x + 1 + k // 8) % 4, (k // 2) % 4, z, k % 2))
+        return carry
+
+    lax.fori_loop(0, 16, greet_column, 0)
+    lax.fori_loop(1, 4, greet_far, 0)
+    lax.fori_loop(1, 64, greet_half, 0)
+    lax.fori_loop(0, 24, greet_plane, 0)
+    pl.semaphore_wait(barrier, 16 + 3 + 63 + 24)
 
     zz = (z + 8 * c) % 16
     home = zz < 8
@@ -138,38 +186,41 @@
         def _():
             relay(a).start()
 
-    def swap_copies(which, j):
+    def swap_copy(which, j, d):
         up4 = (j + zh + 1) % 2
         zt4 = (z + 4 * up4 + 12 * (1 - up4)) % 16
-        copies = []
-        for yt in range(4):
-            where = dev(x, yt, zt4, c)
-            if which == 2:
-                copies.append(remote(meta.at[j], mbuf.at[zh * 4 + y], sw_s.at[2, j, yt], sw_r.at[2], where))
-            else:
-                src = (pot, adj)[which].at[j, :, pl.ds(32 * yt, 32)]
-                dst = (pf, af)[which].at[0, 1 + zh, pl.ds(1 + 2 * y, 2)]
-                copies.append(remote(src, dst, sw_s.at[which, j, yt], sw_r.at[which], where))
-        return copies
-
-    for which in (2, 0, 1):
-        for j in range(2):
-            for copy in swap_copies(which, j):
-                copy.start()
+        yt = (y + d) % 4
+        where = dev(x, yt, zt4, c)
+        if which == 2:
+            return remote(meta.at[j], mbuf.at[zh * 4 + y], sw_s.at[2, j, d], sw_r.at[2], where)
+        src = (pot, adj)[which].at[j, :, pl.ds(pl.multiple_of(32 * yt, 32), 32)]
+        dst = (pf, af)[which].at[0, 1 + zh, pl.ds(1 + 2 * y, 2)]
+        return remote(src, dst, sw_s.at[which, j, d], sw_r.at[which], where)
+
+    def swap_copies(which, j):
+        return [swap_copy(which, j, d) for d in range(4)]
+
+    for j in range(2):
+        for copy in swap_copies(2, j):
+            copy.start()
 
     @pl.when(up + down > 0)
     def _():
         for a in range(5):
             relay(a).wait_send()
 
-    def t_copies(par):
+    def t_x(par):
         return [
             remote(ct.at[par, 8], ct.at[par, 10 * x_last * c], t_s.at[par, 0], t_r.at[par, 0],
                    dev(xn, y, z, (c + x_last) % 2)),
             remote(ct.at[par, 1], ct.at[par, 9 + 2 * x_first * (1 - c)], t_s.at[par, 1], t_r.at[par, 1],
                    dev(xp, y, z, (c + x_first) % 2)),
-            remote(yst.at[par, 0], yct.at[par, 0, y_last], t_s.at[par, 2], t_r.at[par, 2], dev(x, yn, z, c)),
-            remote(yst.at[par, 1], yct.at[par, 1, y_first], t_s.at[par, 3], t_r.at[par, 3], dev(x, yp, z, c)),
+        ]
+
+    def t_y(par):
+        return [
+            remote(yst.at[par, 0], yct.at[par, 0, 0], t_s.at[par, 2], t_r.at[par, 2], dev(x, yn, z, c)),
+            remote(yst.at[par, 1], yct.at[par, 1, 0], t_s.at[par, 3], t_r.at[par, 3], dev(x, yp, z, c)),
         ]
 
     row = iota((32, 128), 0)
@@ -181,76 +232,107 @@
         return below, above
 
     def t_rows(par, p, v):
-        yst[par, 0, pl.ds(p, 1), :] = v[31:32]
-        yst[par, 1, pl.ds(p, 1), :] = v[0:1]
-
-    def first_rows(p, carry):
+        yst[par, 0, p : p + 1, :] = v[31:32]
+        yst[par, 1, p : p + 1, :] = v[0:1]
+
+    for copy in t_x(0):
+        copy.start()
+    for p in range(8):
         t_rows(0, p, ct[0, p + 1])
-        return carry
-
-    lax.fori_loop(0, 8, first_rows, 0)
-    for copy in t_copies(0):
-        copy.start()
-
-    def t_step(s, carry):
-        par = s % 2
+    start_y(t_y(0))
+
+    def t_step(par, last):
         new = 1 - par
-        for copy in t_copies(par):
-            copy.wait()
-
-        def plane(p, inner):
+
+        def plane(p):
             v = ct[par, p + 1]
             xlow = ct[par, p]
             xhigh = ct[par, p + 2]
-            ylow, yhigh = shift_y(v, yct[par, 0, 0, pl.ds(p, 1), :], yct[par, 1, 0, pl.ds(p, 1), :])
+            ylow, yhigh = shift_y(v, yct[par, 0, 0, p : p + 1, :], yct[par, 1, 0, p : p + 1, :])
             zlow = jnp.where(lane == 0, 0.0, pltpu.roll(v, 1, 1))
             zhigh = jnp.where(lane == 127, 0.0, pltpu.roll(v, 127, 1))
-            change = jnp.zeros((32, 128), F32)
+            change = None
             for d, (low, high) in enumerate(((xlow, xhigh), (ylow, yhigh), (zlow, zhigh))):
                 speed = tv[d, p]
-                change = change + jnp.maximum(speed, 0.0) * (v - low) + jnp.minimum(speed, 0.0) * (high - v)
+                term = jnp.maximum(speed, 0.0) * (v - low) + jnp.minimum(speed, 0.0) * (high - v)
+                change = term if change is None else change + term
             v = v - change
             ct[new, p + 1] = v
             t_rows(new, p, v)
-            return inner
-
-        lax.fori_loop(0, 8, plane, 0)
-
-        @pl.when(s < STEPS - 1)
-        def _():
-            for copy in t_copies(new):
+
+        wait_y(t_y(par))
+        for copy in t_x(par):
+            copy.wait()
+        plane(0)
+        plane(7)
+
+        @pl.when(jnp.logical_not(last))
+        def _():
+            for copy in t_x(new):
                 copy.start()
 
+        for p in range(1, 7):
+            plane(p)
+
+        @pl.when(jnp.logical_not(last))
+        def _():
+            start_y(t_y(new))
+
+    def t_two(s, carry):
+        t_step(0, s < 0)
+
+        @pl.when(s < 2)
+        def _():
+            swap_copy(0, s % 2, 0).start()
+            swap_copy(0, s % 2, 1).start()
+
+        @pl.when(s >= 2)
+        def _():
+            swap_copy(1, s % 2, 0).start()
+            swap_copy(1, s % 2, 1).start()
+
+        t_step(1, s == STEPS // 2 - 1)
+
+        @pl.when(s < 2)
+        def _():
+            swap_copy(0, s % 2, 2).start()
+            swap_copy(0, s % 2, 3).start()
+
+        @pl.when(s >= 2)
+        def _():
+            swap_copy(1, s % 2, 2).start()
+            swap_copy(1, s % 2, 3).start()
+
         return carry
 
-    lax.fori_loop(0, STEPS, t_step, 0)
-
-    def conduct(p, carry):
+    lax.fori_loop(0, STEPS // 2, t_two, 0)
+
+    for p in range(8):
         v = jnp.exp(1.8 * jnp.log(tv[3, p])) * (0.5 + ct[0, p + 1])
         sg[1 + c, p + 1] = v
-        yss[0, pl.ds(p, 1), :] = v[31:32]
-        yss[1, pl.ds(p, 1), :] = v[0:1]
-        return carry
-
-    lax.fori_loop(0, 8, conduct, 0)
-
-    def sg_copies():
-        copies = []
-        for cc in range(2):
-            copies += [
-                remote(sg.at[1 + c, 8], sg.at[1 + c + x_last, 0], sg_s.at[0, cc], sg_r.at[0, c], dev(xn, y, z, cc)),
-                remote(sg.at[1 + c, 1], sg.at[1 + c - x_first, 9], sg_s.at[1, cc], sg_r.at[1, c], dev(xp, y, z, cc)),
-                remote(yss.at[0], ysg.at[0, y_last, c], sg_s.at[2, cc], sg_r.at[2, c], dev(x, yn, z, cc)),
-                remote(yss.at[1], ysg.at[1, y_first, c], sg_s.at[3, cc], sg_r.at[3, c], dev(x, yp, z, cc)),
-            ]
-        return copies
+        yss[0, p : p + 1, :] = v[31:32]
+        yss[1, p : p + 1, :] = v[0:1]
+
+    def sg_x(cc):
+        return [
+            remote(sg.at[1 + c, 8], sg.at[1 + c + x_last, 0], sg_s.at[0, cc], sg_r.at[0, c], dev(xn, y, z, cc)),
+            remote(sg.at[1 + c, 1], sg.at[1 + c - x_first, 9], sg_s.at[1, cc], sg_r.at[1, c], dev(xp, y, z, cc)),
+        ]
+
+    def sg_y(cc):
+        return [
+            remote(yss.at[0], ysg.at[0, 0, c], sg_s.at[2, cc], sg_r.at[2, c], dev(x, yn, z, cc)),
+            remote(yss.at[1], ysg.at[1, 0, c], sg_s.at[3, cc], sg_r.at[3, c], dev(x, yp, z, cc)),
+        ]
 
     tile_copy = remote(
         sg.at[1 + c, pl.ds(1, 8)], sg.at[1 + c, pl.ds(1, 8)], tile_s, tile_r, dev(x, y, z, 1 - c)
     )
     tile_copy.start()
-    for copy in sg_copies():
-        copy.start()
+    for cc in range(2):
+        start_y(sg_y(cc))
+        for copy in sg_x(cc):
+            copy.start()
 
     arrived(mbuf, sw_r.at[2])
 
@@ -273,19 +355,25 @@
     jb = mbuf[0, 6:7, :]
 
     tile_copy.wait()
-    for copy in sg_copies():
-        copy.wait_send()
-    for d in range(4):
-        for cc in range(2):
-            if d < 2:
-                arrived(sg.at[1, 0], sg_r.at[d, cc])
-            else:
-                arrived(yss.at[0], sg_r.at[d, cc])
+    for cc in range(2):
+        for d, copy in enumerate(sg_x(cc)):
+            copy.wait_send()
+            arrived(sg.at[1, 0], sg_r.at[d, cc])
+
+        @pl.when(y < 3)
+        def _():
+            sg_y(cc)[0].wait_send()
+            arrived(yss.at[0], sg_r.at[3, cc])
+
+        @pl.when(y > 0)
+        def _():
+            sg_y(cc)[1].wait_send()
+            arrived(yss.at[0], sg_r.at[2, cc])
 
     def faces_of(h, p):
         s = sg[1 + h, p + 1]
-        low = ysg[0, 0, h, pl.ds(p, 1), :]
-        high = ysg[1, 0, h, pl.ds(p, 1), :]
+        low = ysg[0, 0, h, p : p + 1, :]
+        high = ysg[1, 0, h, p : p + 1, :]
         _, syp = shift_y(s, low, high)
         szp = jnp.where(lane == 127, 0.0, pltpu.roll(s, 127, 1))
         ux = harmonic(s, sg[1 + h, p + 2])
@@ -293,8 +381,9 @@
         uz = harmonic(s, szp)
         return s, low, ux, uy, uz
 
-    def coefficients(h):
-        def plane(p, lx):
+    for h in range(2):
+        lx = harmonic(sg[1 + h, 0], sg[1 + h, 1])
+        for p in range(8):
             s, low, ux, uy, uz = faces_of(h, p)
             ly = jnp.where(row == 0, harmonic(low, s[0:1]), pltpu.roll(uy, 1, 0))
             lz = pltpu.roll(uz, 1, 1)
@@ -302,12 +391,7 @@
             rdiag[h, p] = r
             for k, face in enumerate((ux, lx, uy, ly, uz, lz)):
                 coef[k, h, p] = face * r
-            return ux
-
-        lax.fori_loop(0, 8, plane, harmonic(sg[1 + h, 0], sg[1 + h, 1]))
-
-    for h in range(2):
-        coefficients(h)
+            lx = ux
 
     def inject(current):
         vals = dot(jnp.broadcast_to(current, (8, 128)) * own, spread)
@@ -318,58 +402,68 @@
             bsrc[h, pair + 1] = block[32:64] * rdiag[h, pair + 1]
 
     def field(f, yf, ysend, s_sem, r_sem):
-        def copies(par):
+        def x_copies(par):
             return [
                 remote(f.at[par, pl.ds(1, 2), 8], f.at[par, pl.ds(1 + x_last, 2), 0],
                        s_sem.at[par, 0], r_sem.at[par, 0], dev(xn, y, z, c)),
                 remote(f.at[par, pl.ds(1, 2), 1], f.at[par, pl.ds(1 - x_first, 2), 9],
                        s_sem.at[par, 1], r_sem.at[par, 1], dev(xp, y, z, c)),
+            ]
+
+        def y_copies(par):
+            return [
                 remote(ysend.at[par, 0], yf.at[par, 0], s_sem.at[par, 2], r_sem.at[par, 2], dev(x, yn, z, c)),
                 remote(ysend.at[par, 1], yf.at[par, 1], s_sem.at[par, 3], r_sem.at[par, 3], dev(x, yp, z, c)),
             ]
 
         def edge_rows(par, h, p, v):
-            ysend[par, 0, h, pl.ds(p, 1), :] = v[31:32]
-            ysend[par, 1, h, pl.ds(p, 1), :] = v[0:1]
+            ysend[par, 0, h, p : p + 1, :] = v[31:32]
+            ysend[par, 1, h, p : p + 1, :] = v[0:1]
 
         def begin():
+            for copy in x_copies(0):
+                copy.start()
             for h in range(2):
-                def plane(p, carry):
+                for p in range(8):
                     edge_rows(0, h, p, f[0, 1 + h, p + 1])
-                    return carry
-
-                lax.fori_loop(0, 8, plane, 0)
-            for copy in copies(0):
+            start_y(y_copies(0))
+
+        def end(par=0):
+            wait_y(y_copies(par))
+            for copy in x_copies(par):
+                copy.wait()
+
+        def sweep(par):
+            new = 1 - par
+
+            def plane(h, p):
+                v = f[par, 1 + h, p + 1]
+                ylow, yhigh = shift_y(v, yf[par, 0, h, p : p + 1, :], yf[par, 1, h, p : p + 1, :])
+                out = coef[0, h, p] * f[par, 1 + h, p + 2] + coef[1, h, p] * f[par, 1 + h, p]
+                out = out + (coef[2, h, p] * yhigh + coef[3, h, p] * ylow)
+                out = out + (coef[4, h, p] * pltpu.roll(v, 127, 1) + coef[5, h, p] * pltpu.roll(v, 1, 1))
+                out = (0.2 * v + bsrc[h, p]) + out
+                f[new, 1 + h, p + 1] = out
+                edge_rows(new, h, p, out)
+
+            end(par)
+            for p in (0, 7):
+                for h in range(2):
+                    plane(h, p)
+            for copy in x_copies(new):
                 copy.start()
-
-        def sweep(s, carry):
-            par = s % 2
-            new = 1 - par
-            for copy in copies(par):
-                copy.wait()
             for h in range(2):
-                def plane(p, inner):
-                    v = f[par, 1 + h, p + 1]
-                    ylow, yhigh = shift_y(v, yf[par, 0, h, pl.ds(p, 1), :], yf[par, 1, h, pl.ds(p, 1), :])
-                    out = coef[0, h, p] * f[par, 1 + h, p + 2] + coef[1, h, p] * f[par, 1 + h, p]
-                    out = out + (coef[2, h, p] * yhigh + coef[3, h, p] * ylow)
-                    out = out + (coef[4, h, p] * pltpu.roll(v, 127, 1) + coef[5, h, p] * pltpu.roll(v, 1, 1))
-                    out = (0.2 * v + bsrc[h, p]) + out
-                    f[new, 1 + h, p + 1] = out
-                    edge_rows(new, h, p, out)
-                    return inner
-
-                lax.fori_loop(0, 8, plane, 0)
-            for copy in copies(new):
-                copy.start()
+                for p in range(1, 7):
+                    plane(h, p)
+            start_y(y_copies(new))
+
+        def two(s, carry):
+            sweep(0)
+            sweep(1)
             return carry
 
         def sweeps():
-            lax.fori_loop(0, RELAX_SWEEPS, sweep, 0)
-
-        def end():
-            for copy in copies(0):
-                copy.wait()
+            lax.fori_loop(0, RELAX_SWEEPS // 2, two, 0)
 
         return begin, sweeps, end
 
@@ -431,29 +525,23 @@
     a_end()
 
     for h in range(2):
-        def terms(p, carry):
+        for p in range(8):
             _, _, ux, uy, uz = faces_of(h, p)
             pv = pf[0, 1 + h, p + 1]
             av = af[0, 1 + h, p + 1]
-            _, py = shift_y(pv, pv[0:1], ypf[0, 1, h, pl.ds(p, 1), :])
-            _, ay = shift_y(av, av[0:1], yaf[0, 1, h, pl.ds(p, 1), :])
+            _, py = shift_y(pv, pv[0:1], ypf[0, 1, h, p : p + 1, :])
+            _, ay = shift_y(av, av[0:1], yaf[0, 1, h, p : p + 1, :])
             out = ux * (pf[0, 1 + h, p + 2] - pv) * (af[0, 1 + h, p + 2] - av)
             out = out + uy * (py - pv) * (ay - av)
             out = out + uz * (pltpu.roll(pv, 127, 1) - pv) * (pltpu.roll(av, 127, 1) - av)
             gbuf[h, p] = -out
-            return carry
-
-        lax.fori_loop(0, 8, terms, 0)
 
     other = remote(gbuf.at[1 - c], grx, gx_s, gx_r, dev(x, y, z, 1 - c))
     other.start()
     other.wait()
 
-    def pair_sum(p, carry):
+    for p in range(8):
         gsum[p] = gbuf[c, p] + grx[p]
-        return carry
-
-    lax.fori_loop(0, 8, pair_sum, 0)
 
     def rs_copy(k, local):
         p, rh = k // 2, k % 2
@@ -570,7 +658,7 @@
         in_specs=[pl.BlockSpec(memory_space=pl.ANY)] * 4,
         out_specs=(pl.BlockSpec(memory_space=pltpu.VMEM), pl.BlockSpec(memory_space=pltpu.VMEM)),
         scratch_shapes=scratch,
-        compiler_params=pltpu.CompilerParams(has_side_effects=True),
+        compiler_params=pltpu.CompilerParams(collective_id=0, has_side_effects=True),
         name="survey_gradient",
     )(inp, potential_init, adjoint_init, meta)
     return gradient, readings[:, :64]

time: 208 us -> 162 us (0.78)
  Pallas kernels: 199 us -> 154 us
    pallas_call x1, Pallas kernels: 199 us -> 154 us  [on_device(): pl.pallas_call(kernel, out_shape=(jax.ShapeDtypeStruct((2, 128, 128), F32...]
where the time goes in v2:
time: 162 us; the launch traced here: 161 us
  Pallas kernels  154 us (95%)
  local copies, waits for them, and re-layouts  5.07 us (3%)
  other arithmetic  2.09 us (1%)
    pallas_call x1, Pallas kernels, on_device(): pl.pallas_call(kernel, out_shape=(jax.ShapeDtypeStruct((2, 128, 128), F32...  154 us
    unnamed x16, local copies, waits for them, and re-layouts  4.2 us

profile of v2, /device:TPU:17, one launch (start us, length us, event | category | flops | bytes accessed | tf_op | source)
XLA Modules:
  0.0 161.4 jit_solution(2196021523978050943)
XLA Ops:
  0.6 0.0 copy-start
  0.6 0.0 copy-start.1
  0.6 1.0 convert_element_type.35
  1.7 0.0 copy-done
  1.7 0.0 copy-done.1
  1.7 0.0 copy-start.3
  1.7 0.9 pad_maximum_fusion.inp
  2.6 0.0 copy-done.3
  2.6 0.1 reshape.161
  2.7 0.0 copy-start.4
  2.7 0.7 copy-done.4
  3.4 0.0 copy-start.5
  3.4 0.7 copy-done.5
  4.1 0.0 copy-start.2
  4.1 0.7 copy-done.2
  4.8 0.2 convert_reduce_fusion
  5.0 0.1 stack_broadcast_in_dim.12
  5.0 0.1 stack_broadcast_in_dim.26
  5.1 0.6 stack.15.meta
  5.7 153.5 %survey_gradient.1 = (f32[2,128,128]{2,1,0:T(8,128)}, f32[2,128]{1,0:T(2,128)}) custom-call(f32[5,2,128,128]{3,2,1,0:T(8,128)} %pad_maximum_fusion.inp, f32[2,2,128,128]{3,2,1,0:T(8,128)} %pot.1, f32[2,2,128,128]{3,2,1,0:T(8,128)} %adj.1, f32[2,8,128]{2,1,0:T(8,128)} %stack.15.meta), custom_call_target="tpu_custom_call" | custom-call | tf_op jit(solution)/shard_map/survey_gradient/pallas_call | solution.py:655
  159.3 0.0 copy-start.6
  159.3 1.6 copy.13
  160.8 0.0 copy-done.6
  160.8 0.6 copy.14
  (9 shorter events, 0.1 us)
Async XLA Ops:
  0.6 1.0 copy-start
  0.6 1.1 copy-start.1
  1.7 0.9 copy-start.3
  2.7 0.7 copy-start.4
  3.4 0.7 copy-start.5
  4.1 0.7 copy-start.2
  159.3 1.6 copy-start.6

commit v3 on v2

--- a/solution.py
+++ b/solution.py
@@ -8,8 +8,8 @@
 STEPS = 8
 RELAX_SWEEPS = 6
 MESH = pl.DeviceIdType.MESH
-HIGH = lax.Precision.HIGHEST
 F32 = jnp.float32
+BF16 = jnp.bfloat16
 
 
 def harmonic(first, second):
@@ -20,22 +20,37 @@
     return lax.broadcasted_iota(jnp.int32, shape, dim)
 
 
-def dot(a, b):
-    return lax.dot_general(a, b, (((1,), (0,)), ((), ())), precision=HIGH, preferred_element_type=F32)
-
-
-def dot_t(a, b):
-    return lax.dot_general(a, b, (((1,), (1,)), ((), ())), precision=HIGH, preferred_element_type=F32)
+def parts(a):
+    high = a.astype(BF16)
+    rest = a - high.astype(F32)
+    middle = rest.astype(BF16)
+    low = (rest - middle.astype(F32)).astype(BF16)
+    return jnp.concatenate([high, middle, low], axis=0)
+
+
+def total(product):
+    rows = product.shape[0] // 3
+    return product[:rows] + (product[rows : 2 * rows] + product[2 * rows :])
+
+
+def dot(a, exact):
+    dims = (((1,), (0,)), ((), ()))
+    return total(lax.dot_general(parts(a), exact.astype(BF16), dims, preferred_element_type=F32))
+
+
+def dot_t(a, exact):
+    dims = (((1,), (1,)), ((), ()))
+    return total(lax.dot_general(parts(a), exact.astype(BF16), dims, preferred_element_type=F32))
 
 
 def kernel(
-    inp, pot, adj, meta, grad, read,
+    conc, vel, poro, contacts, sources, receivers, observed, pot, adj, grad, read,
     ct, yct, yst, tv, sg, ysg, yss, coef, rdiag, bsrc,
     pf, ypf, ypsend, af, yaf, yasend,
     mbuf, rt, lt, vb, vsend, vall, rsend, rdin,
-    gbuf, grx, gsum, rsbuf, osum,
+    gbuf, grx, gsum, rsbuf, osum, vbf, vf, cin, sin, rin, oin, msend,
     in_s, in_r, rel_s, t_s, t_r, sw_s, sw_r, sg_s, sg_r, tile_s, tile_r,
-    p_s, p_r, a_s, a_r, v_s, v_r, rd_s, rd_r, gx_s, gx_r, rs_s, rs_r, ag_s, ag_r,
+    p_s, p_r, a_s, a_r, v_s, v_r, rd_s, rd_r, gx_s, gx_r, rs_s, rs_r, ag_s, ag_r, fetch,
 ):
     space = lax.axis_index("space")
     tm = lax.axis_index("tm")
@@ -125,45 +140,83 @@
     def greet(where):
         pl.semaphore_signal(barrier, inc=1, device_id=where, device_id_type=MESH)
 
-    def greet_half(k, carry):
-        greet(dev(x, (y + k // 16) % 4, 8 * zh + (zl + (k // 2) % 8) % 8, (c + k % 2) % 2))
-        return carry
-
-    def greet_column(k, carry):
-        greet(dev(x, y, 8 * (1 - zh) + k // 2, k % 2))
-        return carry
-
-    def greet_far(k, carry):
-        greet(dev(x, (y + k) % 4, (z + 4 * (zl // 4) + 12 * (1 - zl // 4)) % 16, c))
+    def greet_row(k, carry):
+        greet(dev(x, (y + k // 2) % 4, z, (c + k % 2) % 2))
         return carry
 
     def greet_plane(k, carry):
         greet(dev((x + 1 + k // 8) % 4, (k // 2) % 4, z, k % 2))
         return carry
 
-    lax.fori_loop(0, 16, greet_column, 0)
+    def greet_column(k, carry):
+        greet(dev(x, y, (z + 1 + k // 2) % 16, k % 2))
+        greet(dev(x, y, (z + 15 - k // 2) % 16, k % 2))
+        return carry
+
+    def greet_far(k, carry):
+        greet(dev(x, (y + k) % 4, (z + 4) % 16, c))
+        greet(dev(x, (y + k) % 4, (z + 12) % 16, c))
+        return carry
+
+    lax.fori_loop(0, 8, greet_column, 0)
     lax.fori_loop(1, 4, greet_far, 0)
-    lax.fori_loop(1, 64, greet_half, 0)
+    lax.fori_loop(1, 8, greet_row, 0)
     lax.fori_loop(0, 24, greet_plane, 0)
-    pl.semaphore_wait(barrier, 16 + 3 + 63 + 24)
+
+    fetched = [
+        pltpu.make_async_copy(a, b, fetch.at[k])
+        for k, (a, b) in enumerate(((vel, vbf), (contacts, cin), (sources, sin), (receivers, rin), (observed, oin)))
+    ]
+    for copy in fetched:
+        copy.start()
+    for copy in fetched:
+        copy.wait()
+    for d in range(3):
+        for p in range(2):
+            vf[d, p] = vbf[d, p].astype(F32)
+    sub = iota((64, 128), 0)
+    col = iota((64, 128), 1)
+    cells = cin[...]
+    q_at = jnp.zeros((16, 128), F32)
+    l_at = jnp.zeros((16, 128), F32)
+    for k in range(4):
+        here = col[0:16] == sub[0:16] + 16 * k
+        q_at = jnp.where(here, (cells[:, k : k + 1] // 128).astype(F32), q_at)
+        l_at = jnp.where(here, (cells[:, k : k + 1] % 128).astype(F32), l_at)
+    used = col[0:1] < 64
+    q_row = jnp.where(used, jnp.sum(q_at, axis=0, keepdims=True), -1.0)
+    l_row = jnp.where(used, jnp.sum(l_at, axis=0, keepdims=True), -1.0)
+    msend[...] = jnp.zeros((2, 8, 128), F32)
+    for j in range(2):
+        msend[j, 0:1, :] = q_row
+        msend[j, 1:2, :] = l_row
+        pairs = rin[j].astype(F32)
+        for k in range(2):
+            at = jnp.where(sub == col, pairs[:, k : k + 1], 0.0)
+            msend[j, 2 + k : 3 + k, :] = jnp.where(used, jnp.sum(at, axis=0, keepdims=True), -1.0)
+            msend[j, 5 + k : 6 + k, :] = jnp.broadcast_to(sin[j : j + 1, k : k + 1].astype(F32), (1, 128))
+        msend[j, 4:5, 0:64] = oin[j : j + 1, :]
+    pl.semaphore_wait(barrier, 16 + 6 + 7 + 24)
 
     zz = (z + 8 * c) % 16
     home = zz < 8
 
-    def landing(a):
-        return ct.at[0, pl.ds(1, 8)] if a == 0 else tv.at[a - 1]
+    def landing(a, g):
+        return ct.at[0, pl.ds(1 + 4 * g, 4)] if a == 0 else tv.at[a - 1, pl.ds(4 * g, 4)]
 
     def landing_two(a):
         return ct.at[0, pl.ds(1 + 2 * y, 2)] if a == 0 else tv.at[a - 1, pl.ds(2 * y, 2)]
 
+    def in_rows(a, yt):
+        rows = pl.ds(pl.multiple_of(32 * yt, 32), 32)
+        return conc.at[:, rows] if a == 0 else poro.at[:, rows] if a == 4 else vf.at[a - 1, :, rows]
+
     def in_copy(a, d):
         yt = (y + d) % 4
-        rows = pl.ds(pl.multiple_of(32 * yt, 32), 32)
-        return remote(inp.at[a, :, rows], landing_two(a), in_s.at[a, d], in_r.at[a], dev(x, yt, z, c))
+        return remote(in_rows(a, yt), landing_two(a), in_s.at[a, d], in_r.at[a, y // 2], dev(x, yt, z, c))
 
     def in_local(a):
-        rows = pl.ds(pl.multiple_of(32 * y, 32), 32)
-        return pltpu.make_async_copy(inp.at[a, :, rows], landing_two(a), in_r.at[a])
+        return pltpu.make_async_copy(in_rows(a, y), landing_two(a), in_r.at[a, y // 2])
 
     @pl.when(home)
     def _():
@@ -176,15 +229,23 @@
     down = jnp.where((zz == 0) | (zz >= 13), 1, 0)
     zt = (z + up + 15 * down) % 16
 
-    def relay(a):
-        return remote(landing(a), landing(a), rel_s.at[a], in_r.at[a], dev(x, y, zt, c))
-
-    for a in range(5):
-        arrived(landing(a), in_r.at[a])
-
+    def relay(a, g):
+        return remote(landing(a, g), landing(a, g), rel_s.at[a, g], in_r.at[a, g], dev(x, y, zt, c))
+
+    def pass_on(a):
+        for g in range(2):
+            arrived(landing(a, g), in_r.at[a, g])
+
+            @pl.when(up + down > 0)
+            def _():
+                relay(a, g).start()
+
+    def passed_on(arrays):
         @pl.when(up + down > 0)
         def _():
-            relay(a).start()
+            for a in arrays:
+                for g in range(2):
+                    relay(a, g).wait_send()
 
     def swap_copy(which, j, d):
         up4 = (j + zh + 1) % 2
@@ -192,22 +253,13 @@
         yt = (y + d) % 4
         where = dev(x, yt, zt4, c)
         if which == 2:
-            return remote(meta.at[j], mbuf.at[zh * 4 + y], sw_s.at[2, j, d], sw_r.at[2], where)
+            return remote(msend.at[j], mbuf.at[zh * 4 + y], sw_s.at[2, j, d], sw_r.at[2], where)
         src = (pot, adj)[which].at[j, :, pl.ds(pl.multiple_of(32 * yt, 32), 32)]
         dst = (pf, af)[which].at[0, 1 + zh, pl.ds(1 + 2 * y, 2)]
         return remote(src, dst, sw_s.at[which, j, d], sw_r.at[which], where)
 
     def swap_copies(which, j):
         return [swap_copy(which, j, d) for d in range(4)]
-
-    for j in range(2):
-        for copy in swap_copies(2, j):
-            copy.start()
-
-    @pl.when(up + down > 0)
-    def _():
-        for a in range(5):
-            relay(a).wait_send()
 
     def t_x(par):
         return [
@@ -235,11 +287,21 @@
         yst[par, 0, p : p + 1, :] = v[31:32]
         yst[par, 1, p : p + 1, :] = v[0:1]
 
+    pass_on(0)
     for copy in t_x(0):
         copy.start()
     for p in range(8):
         t_rows(0, p, ct[0, p + 1])
     start_y(t_y(0))
+    for j in range(2):
+        for copy in swap_copies(2, j):
+            copy.start()
+    for a in range(1, 4):
+        pass_on(a)
+        for d in range(4):
+            if a < 3:
+                swap_copy(0, a - 1, d).start()
+    passed_on([0])
 
     def t_step(par, last):
         new = 1 - par
@@ -281,12 +343,11 @@
     def t_two(s, carry):
         t_step(0, s < 0)
 
+        @pl.when(s == 0)
+        def _():
+            pass_on(4)
+
         @pl.when(s < 2)
-        def _():
-            swap_copy(0, s % 2, 0).start()
-            swap_copy(0, s % 2, 1).start()
-
-        @pl.when(s >= 2)
         def _():
             swap_copy(1, s % 2, 0).start()
             swap_copy(1, s % 2, 1).start()
@@ -295,17 +356,13 @@
 
         @pl.when(s < 2)
         def _():
-            swap_copy(0, s % 2, 2).start()
-            swap_copy(0, s % 2, 3).start()
-
-        @pl.when(s >= 2)
-        def _():
             swap_copy(1, s % 2, 2).start()
             swap_copy(1, s % 2, 3).start()
 
         return carry
 
     lax.fori_loop(0, STEPS // 2, t_two, 0)
+    passed_on(range(1, 5))
 
     for p in range(8):
         v = jnp.exp(1.8 * jnp.log(tv[3, p])) * (0.5 + ct[0, p + 1])
@@ -340,7 +397,7 @@
         q = iota((64, 128), 0)
         target = ((q // 32) * 128 + q % 32 + 32 * y).astype(F32)
         rt[k] = jnp.where(target == mbuf[k, 0:1, :], 1.0, 0.0)
-        lt[k] = jnp.where(iota((128, 128), 0).astype(F32) == mbuf[k, 1:2, :], 1.0, 0.0)
+        lt[k] = jnp.where(iota((128, 128), 0).astype(F32) == mbuf[k, 1:2, :], 1.0, 0.0).astype(BF16)
         return carry
 
     lax.fori_loop(0, 8, tables, 0)
@@ -350,7 +407,7 @@
     own = jnp.where(iota((8, 128), 1) // 16 == iota((8, 128), 0), 1.0, 0.0)
     r0 = mbuf[0, 2:3, :]
     r1 = mbuf[0, 3:4, :]
-    observed = mbuf[0, 4:5, :]
+    measured = mbuf[0, 4:5, :]
     ja = mbuf[0, 5:6, :]
     jb = mbuf[0, 6:7, :]
 
@@ -397,7 +454,7 @@
         vals = dot(jnp.broadcast_to(current, (8, 128)) * own, spread)
         for k in range(8):
             h, pair = k // 4, 2 * (k % 4)
-            block = dot_t(rt[k], lt[k] * vals[k : k + 1, :])
+            block = dot_t(rt[k] * vals[k : k + 1, :], lt[k])
             bsrc[h, pair] = block[0:32] * rdiag[h, pair]
             bsrc[h, pair + 1] = block[32:64] * rdiag[h, pair + 1]
 
@@ -519,29 +576,24 @@
 
     for copy in read_copies():
         copy.start()
-    inject(dot_t(readings - observed, selector(x))[0:1])
+    inject(dot_t(readings - measured, selector(x))[0:1])
     a_sweeps()
     p_end()
     a_end()
 
-    for h in range(2):
-        for p in range(8):
-            _, _, ux, uy, uz = faces_of(h, p)
-            pv = pf[0, 1 + h, p + 1]
-            av = af[0, 1 + h, p + 1]
-            _, py = shift_y(pv, pv[0:1], ypf[0, 1, h, p : p + 1, :])
-            _, ay = shift_y(av, av[0:1], yaf[0, 1, h, p : p + 1, :])
-            out = ux * (pf[0, 1 + h, p + 2] - pv) * (af[0, 1 + h, p + 2] - av)
-            out = out + uy * (py - pv) * (ay - av)
-            out = out + uz * (pltpu.roll(pv, 127, 1) - pv) * (pltpu.roll(av, 127, 1) - av)
-            gbuf[h, p] = -out
-
-    other = remote(gbuf.at[1 - c], grx, gx_s, gx_r, dev(x, y, z, 1 - c))
-    other.start()
-    other.wait()
-
-    for p in range(8):
-        gsum[p] = gbuf[c, p] + grx[p]
+    def terms(h, p):
+        _, _, ux, uy, uz = faces_of(h, p)
+        pv = pf[0, 1 + h, p + 1]
+        av = af[0, 1 + h, p + 1]
+        _, py = shift_y(pv, pv[0:1], ypf[0, 1, h, p : p + 1, :])
+        _, ay = shift_y(av, av[0:1], yaf[0, 1, h, p : p + 1, :])
+        out = ux * (pf[0, 1 + h, p + 2] - pv) * (af[0, 1 + h, p + 2] - av)
+        out = out + uy * (py - pv) * (ay - av)
+        out = out + uz * (pltpu.roll(pv, 127, 1) - pv) * (pltpu.roll(av, 127, 1) - av)
+        return -out
+
+    def other(p):
+        return remote(gbuf.at[p], grx.at[p], gx_s.at[p], gx_r.at[p], dev(x, y, z, 1 - c))
 
     def rs_copy(k, local):
         p, rh = k // 2, k % 2
@@ -554,20 +606,27 @@
     def rs_self(k):
         return (z == 8 * c + k // 2) & (c == k % 2)
 
-    for k in range(16):
-        @pl.when(jnp.logical_not(rs_self(k)))
-        def _():
-            rs_copy(k, False).start()
-
-        @pl.when(rs_self(k))
-        def _():
-            rs_copy(k, True).start()
+    for p in range(8):
+        gbuf[p] = terms(1 - c, p)
+        other(p).start()
+    for p in range(8):
+        mine = terms(c, p)
+        other(p).wait()
+        gsum[p] = mine + grx[p]
+        for k in (2 * p, 2 * p + 1):
+            @pl.when(jnp.logical_not(rs_self(k)))
+            def _():
+                rs_copy(k, False).start()
+
+            @pl.when(rs_self(k))
+            def _():
+                rs_copy(k, True).start()
 
     arrived(rsbuf, rs_r)
-    total = rsbuf[0]
+    added = rsbuf[0]
     for k in range(1, 16):
-        total = total + rsbuf[k]
-    osum[...] = total
+        added = added + rsbuf[k]
+    osum[...] = added
 
     def ag_copy(k, local):
         dst = grad.at[zl % 2, pl.ds(pl.multiple_of(32 * y + 16 * c, 16), 16)]
@@ -588,8 +647,8 @@
             ag_copy(k, True).start()
 
     arrived(rdin, rd_r)
-    read[0:1, :] = rdin[0, 0:1, :]
-    read[1:2, :] = rdin[1, 0:1, :]
+    read[0:1, :] = rdin[0, 0:1, 0:64]
+    read[1:2, :] = rdin[1, 0:1, 0:64]
     arrived(grad, ag_r)
 
     @pl.when(home)
@@ -619,25 +678,6 @@
 def on_device(
     concentration, velocity, porosity, contacts, sources, receivers, observed, potential_init, adjoint_init
 ):
-    inp = jnp.concatenate([concentration[None], velocity.astype(F32), porosity[None]], axis=0)
-    cells = contacts.T.reshape(1, 64)
-    pad = jnp.full((1, 64), -1, jnp.int32)
-    where = jnp.concatenate([cells // 128, pad], axis=1).astype(F32)
-    lanes = jnp.concatenate([cells % 128, pad], axis=1).astype(F32)
-    gap = jnp.full((2, 64), -1.0, F32)
-    meta = jnp.stack(
-        [
-            jnp.broadcast_to(where, (2, 128)),
-            jnp.broadcast_to(lanes, (2, 128)),
-            jnp.concatenate([receivers[:, :, 0].astype(F32), gap], axis=1),
-            jnp.concatenate([receivers[:, :, 1].astype(F32), gap], axis=1),
-            jnp.concatenate([observed, jnp.zeros((2, 64), F32)], axis=1),
-            jnp.broadcast_to(sources[:, 0:1].astype(F32), (2, 128)),
-            jnp.broadcast_to(sources[:, 1:2].astype(F32), (2, 128)),
-            jnp.zeros((2, 128), F32),
-        ],
-        axis=1,
-    )
     V = pltpu.VMEM
     D = pltpu.SemaphoreType.DMA
     scratch = [
@@ -646,22 +686,27 @@
         V((6, 2, 8, 32, 128), F32), V((2, 8, 32, 128), F32), V((2, 8, 32, 128), F32),
         V((2, 4, 10, 32, 128), F32), V((2, 2, 2, 8, 128), F32), V((2, 2, 2, 8, 128), F32),
         V((2, 4, 10, 32, 128), F32), V((2, 2, 2, 8, 128), F32), V((2, 2, 2, 8, 128), F32),
-        V((8, 8, 128), F32), V((8, 64, 128), F32), V((8, 128, 128), F32), V((8, 128), F32), V((8, 128), F32),
+        V((8, 8, 128), F32), V((8, 64, 128), F32), V((8, 128, 128), BF16), V((8, 128), F32), V((8, 128), F32),
         V((16, 8, 128), F32), V((8, 128), F32), V((2, 8, 128), F32),
-        V((2, 8, 32, 128), F32), V((8, 32, 128), F32), V((8, 32, 128), F32), V((16, 16, 128), F32), V((16, 128), F32),
-        D((5, 4)), D((5,)), D((5,)), D((2, 4)), D((2, 4)), D((3, 2, 4)), D((3,)), D((4, 2)), D((4, 2)), D, D,
-        D((2, 4)), D((2, 4)), D((2, 4)), D((2, 4)), D((16,)), D, D((2,)), D, D, D, D((16,)), D, D((16,)), D,
+        V((8, 32, 128), F32), V((8, 32, 128), F32), V((8, 32, 128), F32), V((16, 16, 128), F32), V((16, 128), F32),
+        V((3, 2, 128, 128), BF16), V((3, 2, 128, 128), F32), V((16, 4), jnp.int32), V((2, 2), jnp.int32),
+        V((2, 64, 2), jnp.int32), V((2, 64), F32), V((2, 8, 128), F32),
+        D((5, 4)), D((5, 2)), D((5, 2)), D((2, 4)), D((2, 4)), D((3, 2, 4)), D((3,)), D((4, 2)), D((4, 2)), D, D,
+        D((2, 4)), D((2, 4)), D((2, 4)), D((2, 4)), D((16,)), D, D((2,)), D, D((8,)), D((8,)), D((16,)), D, D((16,)), D,
+        D((5,)),
     ]
     gradient, readings = pl.pallas_call(
         kernel,
-        out_shape=(jax.ShapeDtypeStruct((2, 128, 128), F32), jax.ShapeDtypeStruct((2, 128), F32)),
-        in_specs=[pl.BlockSpec(memory_space=pl.ANY)] * 4,
+        out_shape=(jax.ShapeDtypeStruct((2, 128, 128), F32), jax.ShapeDtypeStruct((2, 64), F32)),
+        in_specs=[pl.BlockSpec(memory_space=pl.ANY)] * 9,
         out_specs=(pl.BlockSpec(memory_space=pltpu.VMEM), pl.BlockSpec(memory_space=pltpu.VMEM)),
         scratch_shapes=scratch,
         compiler_params=pltpu.CompilerParams(collective_id=0, has_side_effects=True),
         name="survey_gradient",
-    )(inp, potential_init, adjoint_init, meta)
-    return gradient, readings[:, :64]
+    )(
+        concentration, velocity, porosity, contacts, sources, receivers, observed, potential_init, adjoint_init
+    )
+    return gradient, readings
 
 
 def solution(mesh):

time: 162 us -> 160 us (0.988)
  other arithmetic: 2.09 us -> 0 us
    unnamed x16 -> x8, local copies, waits for them, and re-layouts: 4.2 us -> 4.23 us
where the time goes in v3:
time: 160 us
  Pallas kernels  155 us (97%)
  local copies, waits for them, and re-layouts  4.23 us (3%)
    pallas_call x1, Pallas kernels, on_device(): pl.pallas_call(kernel, out_shape=(jax.ShapeDtypeStruct((2, 128, 128), F32...  155 us
    unnamed x8, local copies, waits for them, and re-layouts  4.23 us

profile of v3, /device:TPU:17, one launch (start us, length us, event | category | flops | bytes accessed | tf_op | source)
XLA Modules:
  0.0 159.8 jit_solution(13362542637487594107)
XLA Ops:
  0.6 0.0 copy-start
  0.6 1.4 copy.11.contacts
  2.0 0.0 copy-done
  2.0 0.7 copy.12.receivers
  2.7 154.9 %survey_gradient.1 = (f32[2,128,128]{2,1,0:T(8,128)}, f32[2,64]{1,0:T(2,128)}) custom-call(f32[2,128,128]{2,1,0:T(8,128)} %conc.1, bf16[3,2,128,128]{3,2,1,0:T(8,128)(2,1)} %vel.1, f32[2,128,128]{2,1,0:T(8,128)} %poro.1, s32[16,4]{1,0:T(8,128)} %copy.11.contacts, s32[2,2]{1,0:T(2,128)} %sources.1, s32[2,64,2]{2,1,0:T(8,128)} %copy.12.receivers, ...), custom_call_target="tpu_custom_call" | custom-call | tf_op jit(solution)/shard_map/survey_gradient/pallas_call | solution.py:698
  157.6 0.0 copy-start.1
  157.7 1.6 copy.15
  159.2 0.0 copy-done.1
  159.2 0.6 copy.16
Async XLA Ops:
  0.6 1.4 copy-start
  157.6 1.6 copy-start.1

commit v4 on v3

--- a/solution.py
+++ b/solution.py
@@ -174,78 +174,21 @@
     for d in range(3):
         for p in range(2):
             vf[d, p] = vbf[d, p].astype(F32)
-    sub = iota((64, 128), 0)
-    col = iota((64, 128), 1)
     cells = cin[...]
-    q_at = jnp.zeros((16, 128), F32)
-    l_at = jnp.zeros((16, 128), F32)
-    for k in range(4):
-        here = col[0:16] == sub[0:16] + 16 * k
-        q_at = jnp.where(here, (cells[:, k : k + 1] // 128).astype(F32), q_at)
-        l_at = jnp.where(here, (cells[:, k : k + 1] % 128).astype(F32), l_at)
-    used = col[0:1] < 64
-    q_row = jnp.where(used, jnp.sum(q_at, axis=0, keepdims=True), -1.0)
-    l_row = jnp.where(used, jnp.sum(l_at, axis=0, keepdims=True), -1.0)
     msend[...] = jnp.zeros((2, 8, 128), F32)
     for j in range(2):
-        msend[j, 0:1, :] = q_row
-        msend[j, 1:2, :] = l_row
-        pairs = rin[j].astype(F32)
+        msend[j, 0:4, :] = jnp.full((4, 128), -1.0, F32)
+        for k in range(4):
+            msend[j, 0:1, 16 * k : 16 * k + 16] = (cells[k : k + 1] // 128).astype(F32)
+            msend[j, 1:2, 16 * k : 16 * k + 16] = (cells[k : k + 1] % 128).astype(F32)
         for k in range(2):
-            at = jnp.where(sub == col, pairs[:, k : k + 1], 0.0)
-            msend[j, 2 + k : 3 + k, :] = jnp.where(used, jnp.sum(at, axis=0, keepdims=True), -1.0)
+            msend[j, 2 + k : 3 + k, 0:64] = rin[j, k : k + 1, :].astype(F32)
             msend[j, 5 + k : 6 + k, :] = jnp.broadcast_to(sin[j : j + 1, k : k + 1].astype(F32), (1, 128))
         msend[j, 4:5, 0:64] = oin[j : j + 1, :]
     pl.semaphore_wait(barrier, 16 + 6 + 7 + 24)
 
     zz = (z + 8 * c) % 16
     home = zz < 8
-
-    def landing(a, g):
-        return ct.at[0, pl.ds(1 + 4 * g, 4)] if a == 0 else tv.at[a - 1, pl.ds(4 * g, 4)]
-
-    def landing_two(a):
-        return ct.at[0, pl.ds(1 + 2 * y, 2)] if a == 0 else tv.at[a - 1, pl.ds(2 * y, 2)]
-
-    def in_rows(a, yt):
-        rows = pl.ds(pl.multiple_of(32 * yt, 32), 32)
-        return conc.at[:, rows] if a == 0 else poro.at[:, rows] if a == 4 else vf.at[a - 1, :, rows]
-
-    def in_copy(a, d):
-        yt = (y + d) % 4
-        return remote(in_rows(a, yt), landing_two(a), in_s.at[a, d], in_r.at[a, y // 2], dev(x, yt, z, c))
-
-    def in_local(a):
-        return pltpu.make_async_copy(in_rows(a, y), landing_two(a), in_r.at[a, y // 2])
-
-    @pl.when(home)
-    def _():
-        for a in range(5):
-            for d in range(1, 4):
-                in_copy(a, d).start()
-            in_local(a).start()
-
-    up = jnp.where((zz >= 7) & (zz <= 10), 1, 0)
-    down = jnp.where((zz == 0) | (zz >= 13), 1, 0)
-    zt = (z + up + 15 * down) % 16
-
-    def relay(a, g):
-        return remote(landing(a, g), landing(a, g), rel_s.at[a, g], in_r.at[a, g], dev(x, y, zt, c))
-
-    def pass_on(a):
-        for g in range(2):
-            arrived(landing(a, g), in_r.at[a, g])
-
-            @pl.when(up + down > 0)
-            def _():
-                relay(a, g).start()
-
-    def passed_on(arrays):
-        @pl.when(up + down > 0)
-        def _():
-            for a in arrays:
-                for g in range(2):
-                    relay(a, g).wait_send()
 
     def swap_copy(which, j, d):
         up4 = (j + zh + 1) % 2
@@ -260,6 +203,56 @@
 
     def swap_copies(which, j):
         return [swap_copy(which, j, d) for d in range(4)]
+
+    def landing(a, g):
+        return ct.at[0, pl.ds(1 + 4 * g, 4)] if a == 0 else tv.at[a - 1, pl.ds(4 * g, 4)]
+
+    def landing_two(a):
+        return ct.at[0, pl.ds(1 + 2 * y, 2)] if a == 0 else tv.at[a - 1, pl.ds(2 * y, 2)]
+
+    def in_rows(a, yt):
+        rows = pl.ds(pl.multiple_of(32 * yt, 32), 32)
+        return conc.at[:, rows] if a == 0 else poro.at[:, rows] if a == 4 else vf.at[a - 1, :, rows]
+
+    def in_copy(a, d):
+        yt = (y + d) % 4
+        return remote(in_rows(a, yt), landing_two(a), in_s.at[a, d], in_r.at[a, y // 2], dev(x, yt, z, c))
+
+    def in_local(a):
+        return pltpu.make_async_copy(in_rows(a, y), landing_two(a), in_r.at[a, y // 2])
+
+    @pl.when(home)
+    def _():
+        for a in range(5):
+            for d in range(1, 4):
+                in_copy(a, d).start()
+            in_local(a).start()
+
+    for j in range(2):
+        for d in range(4):
+            swap_copy(0, j, d).start()
+
+    up = jnp.where((zz >= 7) & (zz <= 10), 1, 0)
+    down = jnp.where((zz == 0) | (zz >= 13), 1, 0)
+    zt = (z + up + 15 * down) % 16
+
+    def relay(a, g):
+        return remote(landing(a, g), landing(a, g), rel_s.at[a, g], in_r.at[a, g], dev(x, y, zt, c))
+
+    def pass_on(a):
+        for g in range(2):
+            arrived(landing(a, g), in_r.at[a, g])
+
+            @pl.when(up + down > 0)
+            def _():
+                relay(a, g).start()
+
+    def passed_on(arrays):
+        @pl.when(up + down > 0)
+        def _():
+            for a in arrays:
+                for g in range(2):
+                    relay(a, g).wait_send()
 
     def t_x(par):
         return [
@@ -298,9 +291,6 @@
             copy.start()
     for a in range(1, 4):
         pass_on(a)
-        for d in range(4):
-            if a < 3:
-                swap_copy(0, a - 1, d).start()
     passed_on([0])
 
     def t_step(par, last):
@@ -347,17 +337,7 @@
         def _():
             pass_on(4)
 
-        @pl.when(s < 2)
-        def _():
-            swap_copy(1, s % 2, 0).start()
-            swap_copy(1, s % 2, 1).start()
-
         t_step(1, s == STEPS // 2 - 1)
-
-        @pl.when(s < 2)
-        def _():
-            swap_copy(1, s % 2, 2).start()
-            swap_copy(1, s % 2, 3).start()
 
         return carry
 
@@ -390,6 +370,9 @@
         start_y(sg_y(cc))
         for copy in sg_x(cc):
             copy.start()
+    for j in range(2):
+        for d in range(4):
+            swap_copy(1, j, d).start()
 
     arrived(mbuf, sw_r.at[2])
 
@@ -689,8 +672,8 @@
         V((8, 8, 128), F32), V((8, 64, 128), F32), V((8, 128, 128), BF16), V((8, 128), F32), V((8, 128), F32),
         V((16, 8, 128), F32), V((8, 128), F32), V((2, 8, 128), F32),
         V((8, 32, 128), F32), V((8, 32, 128), F32), V((8, 32, 128), F32), V((16, 16, 128), F32), V((16, 128), F32),
-        V((3, 2, 128, 128), BF16), V((3, 2, 128, 128), F32), V((16, 4), jnp.int32), V((2, 2), jnp.int32),
-        V((2, 64, 2), jnp.int32), V((2, 64), F32), V((2, 8, 128), F32),
+        V((3, 2, 128, 128), BF16), V((3, 2, 128, 128), F32), V((4, 16), jnp.int32), V((2, 2), jnp.int32),
+        V((2, 2, 64), jnp.int32), V((2, 64), F32), V((2, 8, 128), F32),
         D((5, 4)), D((5, 2)), D((5, 2)), D((2, 4)), D((2, 4)), D((3, 2, 4)), D((3,)), D((4, 2)), D((4, 2)), D, D,
         D((2, 4)), D((2, 4)), D((2, 4)), D((2, 4)), D((16,)), D, D((2,)), D, D((8,)), D((8,)), D((16,)), D, D((16,)), D,
         D((5,)),
@@ -704,7 +687,8 @@
         compiler_params=pltpu.CompilerParams(collective_id=0, has_side_effects=True),
         name="survey_gradient",
     )(
-        concentration, velocity, porosity, contacts, sources, receivers, observed, potential_init, adjoint_init
+        concentration, velocity, porosity, contacts.T, sources, jnp.swapaxes(receivers, 1, 2), observed,
+        potential_init, adjoint_init,
     )
     return gradient, readings
 

time: 160 us -> 144 us (0.900)
  Pallas kernels: 155 us -> 141 us
  local copies, waits for them, and re-layouts: 4.23 us -> 2.14 us
    pallas_call x1, Pallas kernels: 155 us -> 141 us  [on_device(): pl.pallas_call(kernel, out_shape=(jax.ShapeDtypeStruct((2, 128, 128), F32...]
    unnamed x8 -> x4, local copies, waits for them, and re-layouts: 4.23 us -> 2.14 us
where the time goes in v4:
time: 144 us
  Pallas kernels  141 us (98%)
  local copies, waits for them, and re-layouts  2.14 us (1%)
    pallas_call x1, Pallas kernels, on_device(): pl.pallas_call(kernel, out_shape=(jax.ShapeDtypeStruct((2, 128, 128), F32...  141 us

profile of v4, /device:TPU:17, one launch (start us, length us, event | category | flops | bytes accessed | tf_op | source)
XLA Modules:
  0.0 143.5 jit_solution(11468786341032722554)
XLA Ops:
  0.6 140.7 %survey_gradient.1 = (f32[2,128,128]{2,1,0:T(8,128)}, f32[2,64]{1,0:T(2,128)}) custom-call(f32[2,128,128]{2,1,0:T(8,128)} %conc.1, bf16[3,2,128,128]{3,2,1,0:T(8,128)(2,1)} %vel.1, f32[2,128,128]{2,1,0:T(8,128)} %poro.1, s32[4,16]{1,0:T(4,128)} %bitcast.2, s32[2,2]{1,0:T(2,128)} %sources.1, s32[2,2,64]{2,1,0:T(2,128)} %bitcast.3, f32[2,64]{1,0:T(2,128)} %observed.1, ...), custom_call_target="tpu_custom_call" | custom-call | tf_op jit(solution)/shard_map/survey_gradient/pallas_call | solution.py:681
  141.4 0.0 copy-start
  141.4 1.6 %copy.13 = f32[2,128,128]{2,1,0:T(8,128)} copy(f32[2,128,128]{2,1,0:T(8,128)} %get-tuple-element.4) | data formatting | bytes 262144
  143.0 0.0 copy-done
  143.0 0.6 copy.14
Async XLA Ops:
  141.4 1.6 %copy-start = (f32[2,64]{1,0:T(2,128)S(1)}, f32[2,64]{1,0:T(2,128)}, u32[]{:S(2)}) copy-start(f32[2,64]{1,0:T(2,128)} %get-tuple-element.5) | copy-start | bytes 1540

commit v5 on v4

--- a/solution.py
+++ b/solution.py
@@ -49,7 +49,7 @@
     pf, ypf, ypsend, af, yaf, yasend,
     mbuf, rt, lt, vb, vsend, vall, rsend, rdin,
     gbuf, grx, gsum, rsbuf, osum, vbf, vf, cin, sin, rin, oin, msend,
-    in_s, in_r, rel_s, t_s, t_r, sw_s, sw_r, sg_s, sg_r, tile_s, tile_r,
+    in_s, out_s, in_r, rel_s, t_s, t_r, sw_s, sw_r, sg_s, sg_r, tile_s, tile_r,
     p_s, p_r, a_s, a_r, v_s, v_r, rd_s, rd_r, gx_s, gx_r, rs_s, rs_r, ag_s, ag_r, fetch,
 ):
     space = lax.axis_index("space")
@@ -156,6 +156,8 @@
     def greet_far(k, carry):
         greet(dev(x, (y + k) % 4, (z + 4) % 16, c))
         greet(dev(x, (y + k) % 4, (z + 12) % 16, c))
+        greet(dev(x, (y + k) % 4, (z + 1) % 16, c))
+        greet(dev(x, (y + k) % 4, (z + 15) % 16, c))
         return carry
 
     lax.fori_loop(0, 8, greet_column, 0)
@@ -185,7 +187,7 @@
             msend[j, 2 + k : 3 + k, 0:64] = rin[j, k : k + 1, :].astype(F32)
             msend[j, 5 + k : 6 + k, :] = jnp.broadcast_to(sin[j : j + 1, k : k + 1].astype(F32), (1, 128))
         msend[j, 4:5, 0:64] = oin[j : j + 1, :]
-    pl.semaphore_wait(barrier, 16 + 6 + 7 + 24)
+    pl.semaphore_wait(barrier, 16 + 12 + 7 + 24)
 
     zz = (z + 8 * c) % 16
     home = zz < 8
@@ -218,24 +220,34 @@
         yt = (y + d) % 4
         return remote(in_rows(a, yt), landing_two(a), in_s.at[a, d], in_r.at[a, y // 2], dev(x, yt, z, c))
 
+    up = jnp.where((zz >= 7) & (zz <= 10), 1, 0)
+    down = jnp.where((zz == 0) | (zz >= 13), 1, 0)
+    zt = (z + up + 15 * down) % 16
+    passing = (up + down > 0) & (zz >= 8)
+    leaving = (zz == 7) | (zz == 0)
+
+    def out_copy(a, d):
+        yt = (y + d) % 4
+        return remote(in_rows(a, yt), landing_two(a), out_s.at[a, d], in_r.at[a, y // 2], dev(x, yt, zt, c))
+
     def in_local(a):
         return pltpu.make_async_copy(in_rows(a, y), landing_two(a), in_r.at[a, y // 2])
 
     @pl.when(home)
     def _():
         for a in range(5):
+            @pl.when(leaving)
+            def _():
+                for d in range(4):
+                    out_copy(a, d).start()
+
             for d in range(1, 4):
                 in_copy(a, d).start()
             in_local(a).start()
 
     for j in range(2):
-        for d in range(4):
-            swap_copy(0, j, d).start()
-
-    up = jnp.where((zz >= 7) & (zz <= 10), 1, 0)
-    down = jnp.where((zz == 0) | (zz >= 13), 1, 0)
-    zt = (z + up + 15 * down) % 16
-
+        for copy in swap_copies(2, j):
+            copy.start()
     def relay(a, g):
         return remote(landing(a, g), landing(a, g), rel_s.at[a, g], in_r.at[a, g], dev(x, y, zt, c))
 
@@ -243,12 +255,12 @@
         for g in range(2):
             arrived(landing(a, g), in_r.at[a, g])
 
-            @pl.when(up + down > 0)
+            @pl.when(passing)
             def _():
                 relay(a, g).start()
 
     def passed_on(arrays):
-        @pl.when(up + down > 0)
+        @pl.when(passing)
         def _():
             for a in arrays:
                 for g in range(2):
@@ -287,8 +299,8 @@
         t_rows(0, p, ct[0, p + 1])
     start_y(t_y(0))
     for j in range(2):
-        for copy in swap_copies(2, j):
-            copy.start()
+        for d in range(4):
+            swap_copy(0, j, d).start()
     for a in range(1, 4):
         pass_on(a)
     passed_on([0])
@@ -330,14 +342,24 @@
         def _():
             start_y(t_y(new))
 
+    def tables(k):
+        q = iota((64, 128), 0)
+        target = ((q // 32) * 128 + q % 32 + 32 * y).astype(F32)
+        rt[k] = jnp.where(target == mbuf[k, 0:1, :], 1.0, 0.0)
+        lt[k] = jnp.where(iota((128, 128), 0).astype(F32) == mbuf[k, 1:2, :], 1.0, 0.0).astype(BF16)
+
+    arrived(mbuf, sw_r.at[2])
+
     def t_two(s, carry):
         t_step(0, s < 0)
+        tables(2 * s)
 
         @pl.when(s == 0)
         def _():
             pass_on(4)
 
         t_step(1, s == STEPS // 2 - 1)
+        tables(2 * s + 1)
 
         return carry
 
@@ -374,16 +396,6 @@
         for d in range(4):
             swap_copy(1, j, d).start()
 
-    arrived(mbuf, sw_r.at[2])
-
-    def tables(k, carry):
-        q = iota((64, 128), 0)
-        target = ((q // 32) * 128 + q % 32 + 32 * y).astype(F32)
-        rt[k] = jnp.where(target == mbuf[k, 0:1, :], 1.0, 0.0)
-        lt[k] = jnp.where(iota((128, 128), 0).astype(F32) == mbuf[k, 1:2, :], 1.0, 0.0).astype(BF16)
-        return carry
-
-    lax.fori_loop(0, 8, tables, 0)
     jj = iota((128, 128), 0)
     mm = iota((128, 128), 1)
     spread = jnp.where((jj % 16 == mm % 16) & (mm < 64), 0.25, 0.0)
@@ -394,6 +406,89 @@
     ja = mbuf[0, 5:6, :]
     jb = mbuf[0, 6:7, :]
 
+    def inject(current, finish):
+        vals = dot(jnp.broadcast_to(current, (8, 128)) * own, spread)
+        for k in range(8):
+            h, pair = k // 4, 2 * (k % 4)
+            block = dot_t(rt[k] * vals[k : k + 1, :], lt[k])
+            for n in range(2):
+                rows = block[32 * n : 32 * n + 32]
+                bsrc[h, pair + n] = rows * rdiag[h, pair + n] if finish else rows
+
+    def field(f, yf, ysend, s_sem, r_sem):
+        def x_copies(par):
+            return [
+                remote(f.at[par, pl.ds(1, 2), 8], f.at[par, pl.ds(1 + x_last, 2), 0],
+                       s_sem.at[par, 0], r_sem.at[par, 0], dev(xn, y, z, c)),
+                remote(f.at[par, pl.ds(1, 2), 1], f.at[par, pl.ds(1 - x_first, 2), 9],
+                       s_sem.at[par, 1], r_sem.at[par, 1], dev(xp, y, z, c)),
+            ]
+
+        def y_copies(par):
+            return [
+                remote(ysend.at[par, 0], yf.at[par, 0], s_sem.at[par, 2], r_sem.at[par, 2], dev(x, yn, z, c)),
+                remote(ysend.at[par, 1], yf.at[par, 1], s_sem.at[par, 3], r_sem.at[par, 3], dev(x, yp, z, c)),
+            ]
+
+        def edge_rows(par, h, p, v):
+            ysend[par, 0, h, p : p + 1, :] = v[31:32]
+            ysend[par, 1, h, p : p + 1, :] = v[0:1]
+
+        def begin():
+            for copy in x_copies(0):
+                copy.start()
+            for h in range(2):
+                for p in range(8):
+                    edge_rows(0, h, p, f[0, 1 + h, p + 1])
+            start_y(y_copies(0))
+
+        def end(par=0):
+            wait_y(y_copies(par))
+            for copy in x_copies(par):
+                copy.wait()
+
+        def sweep(par):
+            new = 1 - par
+
+            def plane(h, p):
+                v = f[par, 1 + h, p + 1]
+                ylow, yhigh = shift_y(v, yf[par, 0, h, p : p + 1, :], yf[par, 1, h, p : p + 1, :])
+                out = coef[0, h, p] * f[par, 1 + h, p + 2] + coef[1, h, p] * f[par, 1 + h, p]
+                out = out + (coef[2, h, p] * yhigh + coef[3, h, p] * ylow)
+                out = out + (coef[4, h, p] * pltpu.roll(v, 127, 1) + coef[5, h, p] * pltpu.roll(v, 1, 1))
+                out = (0.2 * v + bsrc[h, p]) + out
+                f[new, 1 + h, p + 1] = out
+                edge_rows(new, h, p, out)
+
+            end(par)
+            for p in (0, 7):
+                for h in range(2):
+                    plane(h, p)
+            for copy in x_copies(new):
+                copy.start()
+            for h in range(2):
+                for p in range(1, 7):
+                    plane(h, p)
+            start_y(y_copies(new))
+
+        def two(s, carry):
+            sweep(0)
+            sweep(1)
+            return carry
+
+        def sweeps():
+            lax.fori_loop(0, RELAX_SWEEPS // 2, two, 0)
+
+        return begin, sweeps, end
+
+    own_lane = iota((1, 128), 1)
+    own_ids = ((own_lane // 64) * 256 + x * 64 + own_lane % 64).astype(F32)
+    inject(4.0 * (jnp.where(own_ids == ja, 1.0, 0.0) - jnp.where(own_ids == jb, 1.0, 0.0)), False)
+
+    p_begin, p_sweeps, p_end = field(pf, ypf, ypsend, p_s, p_r)
+    a_begin, a_sweeps, a_end = field(af, yaf, yasend, a_s, a_r)
+    arrived(pf.at[0, pl.ds(1, 2), pl.ds(1, 8)], sw_r.at[0])
+    p_begin()
     tile_copy.wait()
     for cc in range(2):
         for d, copy in enumerate(sg_x(cc)):
@@ -429,96 +524,15 @@
             lz = pltpu.roll(uz, 1, 1)
             r = 0.8 / (ux + lx + uy + ly + uz + lz)
             rdiag[h, p] = r
+            bsrc[h, p] = bsrc[h, p] * r
             for k, face in enumerate((ux, lx, uy, ly, uz, lz)):
                 coef[k, h, p] = face * r
             lx = ux
 
-    def inject(current):
-        vals = dot(jnp.broadcast_to(current, (8, 128)) * own, spread)
-        for k in range(8):
-            h, pair = k // 4, 2 * (k % 4)
-            block = dot_t(rt[k] * vals[k : k + 1, :], lt[k])
-            bsrc[h, pair] = block[0:32] * rdiag[h, pair]
-            bsrc[h, pair + 1] = block[32:64] * rdiag[h, pair + 1]
-
-    def field(f, yf, ysend, s_sem, r_sem):
-        def x_copies(par):
-            return [
-                remote(f.at[par, pl.ds(1, 2), 8], f.at[par, pl.ds(1 + x_last, 2), 0],
-                       s_sem.at[par, 0], r_sem.at[par, 0], dev(xn, y, z, c)),
-                remote(f.at[par, pl.ds(1, 2), 1], f.at[par, pl.ds(1 - x_first, 2), 9],
-                       s_sem.at[par, 1], r_sem.at[par, 1], dev(xp, y, z, c)),
-            ]
-
-        def y_copies(par):
-            return [
-                remote(ysend.at[par, 0], yf.at[par, 0], s_sem.at[par, 2], r_sem.at[par, 2], dev(x, yn, z, c)),
-                remote(ysend.at[par, 1], yf.at[par, 1], s_sem.at[par, 3], r_sem.at[par, 3], dev(x, yp, z, c)),
-            ]
-
-        def edge_rows(par, h, p, v):
-            ysend[par, 0, h, p : p + 1, :] = v[31:32]
-            ysend[par, 1, h, p : p + 1, :] = v[0:1]
-
-        def begin():
-            for copy in x_copies(0):
-                copy.start()
-            for h in range(2):
-                for p in range(8):
-                    edge_rows(0, h, p, f[0, 1 + h, p + 1])
-            start_y(y_copies(0))
-
-        def end(par=0):
-            wait_y(y_copies(par))
-            for copy in x_copies(par):
-                copy.wait()
-
-        def sweep(par):
-            new = 1 - par
-
-            def plane(h, p):
-                v = f[par, 1 + h, p + 1]
-                ylow, yhigh = shift_y(v, yf[par, 0, h, p : p + 1, :], yf[par, 1, h, p : p + 1, :])
-                out = coef[0, h, p] * f[par, 1 + h, p + 2] + coef[1, h, p] * f[par, 1 + h, p]
-                out = out + (coef[2, h, p] * yhigh + coef[3, h, p] * ylow)
-                out = out + (coef[4, h, p] * pltpu.roll(v, 127, 1) + coef[5, h, p] * pltpu.roll(v, 1, 1))
-                out = (0.2 * v + bsrc[h, p]) + out
-                f[new, 1 + h, p + 1] = out
-                edge_rows(new, h, p, out)
-
-            end(par)
-            for p in (0, 7):
-                for h in range(2):
-                    plane(h, p)
-            for copy in x_copies(new):
-                copy.start()
-            for h in range(2):
-                for p in range(1, 7):
-                    plane(h, p)
-            start_y(y_copies(new))
-
-        def two(s, carry):
-            sweep(0)
-            sweep(1)
-            return carry
-
-        def sweeps():
-            lax.fori_loop(0, RELAX_SWEEPS // 2, two, 0)
-
-        return begin, sweeps, end
-
     def electrode_ids(x_):
         j = iota((128, 128), 0)
         return ((j // 64) * 256 + x_ * 64 + j % 64).astype(F32)
 
-    own_lane = iota((1, 128), 1)
-    own_ids = ((own_lane // 64) * 256 + x * 64 + own_lane % 64).astype(F32)
-    inject(4.0 * (jnp.where(own_ids == ja, 1.0, 0.0) - jnp.where(own_ids == jb, 1.0, 0.0)))
-
-    p_begin, p_sweeps, p_end = field(pf, ypf, ypsend, p_s, p_r)
-    a_begin, a_sweeps, a_end = field(af, yaf, yasend, a_s, a_r)
-    arrived(pf.at[0, pl.ds(1, 2), pl.ds(1, 8)], sw_r.at[0])
-    p_begin()
     p_sweeps()
 
     for k in range(8):
@@ -559,7 +573,7 @@
 
     for copy in read_copies():
         copy.start()
-    inject(dot_t(readings - measured, selector(x))[0:1])
+    inject(dot_t(readings - measured, selector(x))[0:1], True)
     a_sweeps()
     p_end()
     a_end()
@@ -615,10 +629,13 @@
         dst = grad.at[zl % 2, pl.ds(pl.multiple_of(32 * y + 16 * c, 16), 16)]
         if local:
             return pltpu.make_async_copy(osum, dst, ag_r)
-        return remote(osum, dst, ag_s.at[k], ag_r, dev(x, zl // 2, 8 * zh + k // 2, k % 2))
+        return remote(osum, dst, ag_s.at[k], ag_r, dev(x, zl // 2, 8 * zh + ag_z(k), k % 2))
+
+    def ag_z(k):
+        return (k // 2) * (zl // 4) + (7 - k // 2) * (1 - zl // 4)
 
     def ag_self(k):
-        return (y == zl // 2) & (zl == k // 2) & (c == k % 2)
+        return (y == zl // 2) & (zl == ag_z(k)) & (c == k % 2)
 
     for k in range(16):
         @pl.when(jnp.logical_not(ag_self(k)))
@@ -639,6 +656,12 @@
         for a in range(5):
             for d in range(1, 4):
                 in_copy(a, d).wait_send()
+
+            @pl.when(leaving)
+            def _():
+                for d in range(4):
+                    out_copy(a, d).wait_send()
+
 
     for which in range(3):
         for j in range(2):
@@ -674,7 +697,7 @@
         V((8, 32, 128), F32), V((8, 32, 128), F32), V((8, 32, 128), F32), V((16, 16, 128), F32), V((16, 128), F32),
         V((3, 2, 128, 128), BF16), V((3, 2, 128, 128), F32), V((4, 16), jnp.int32), V((2, 2), jnp.int32),
         V((2, 2, 64), jnp.int32), V((2, 64), F32), V((2, 8, 128), F32),
-        D((5, 4)), D((5, 2)), D((5, 2)), D((2, 4)), D((2, 4)), D((3, 2, 4)), D((3,)), D((4, 2)), D((4, 2)), D, D,
+        D((5, 4)), D((5, 4)), D((5, 2)), D((5, 2)), D((2, 4)), D((2, 4)), D((3, 2, 4)), D((3,)), D((4, 2)), D((4, 2)), D, D,
         D((2, 4)), D((2, 4)), D((2, 4)), D((2, 4)), D((16,)), D, D((2,)), D, D((8,)), D((8,)), D((16,)), D, D((16,)), D,
         D((5,)),
     ]

time: 144 us -> 141 us (0.979)
  Pallas kernels: 141 us -> 139 us
    pallas_call x1, Pallas kernels: 141 us -> 139 us  [on_device(): pl.pallas_call(kernel, out_shape=(jax.ShapeDtypeStruct((2, 128, 128), F32...]
where the time goes in v5:
time: 141 us
  Pallas kernels  139 us (99%)
  local copies, waits for them, and re-layouts  2.14 us (2%)
    pallas_call x1, Pallas kernels, on_device(): pl.pallas_call(kernel, out_shape=(jax.ShapeDtypeStruct((2, 128, 128), F32...  139 us

profile of v5, /device:TPU:17, one launch (start us, length us, event | category | flops | bytes accessed | tf_op | source)
XLA Modules:
  0.0 141.3 jit_solution(1180339471594062151)
XLA Ops:
  0.6 138.5 %survey_gradient.1 = (f32[2,128,128]{2,1,0:T(8,128)}, f32[2,64]{1,0:T(2,128)}) custom-call(f32[2,128,128]{2,1,0:T(8,128)} %conc.1, bf16[3,2,128,128]{3,2,1,0:T(8,128)(2,1)} %vel.1, f32[2,128,128]{2,1,0:T(8,128)} %poro.1, s32[4,16]{1,0:T(4,128)} %bitcast.2, s32[2,2]{1,0:T(2,128)} %sources.1, s32[2,2,64]{2,1,0:T(2,128)} %bitcast.3, f32[2,64]{1,0:T(2,128)} %observed.1, ...), custom_call_target="tpu_custom_call" | custom-call | tf_op jit(solution)/shard_map/survey_gradient/pallas_call | solution.py:704
  139.2 0.0 copy-start
  139.2 1.6 %copy.13 = f32[2,128,128]{2,1,0:T(8,128)} copy(f32[2,128,128]{2,1,0:T(8,128)} %get-tuple-element.4) | data formatting | bytes 262144
  140.8 0.0 copy-done
  140.8 0.6 copy.14
Async XLA Ops:
  139.2 1.6 %copy-start = (f32[2,64]{1,0:T(2,128)S(1)}, f32[2,64]{1,0:T(2,128)}, u32[]{:S(2)}) copy-start(f32[2,64]{1,0:T(2,128)} %get-tuple-element.5) | copy-start | bytes 1540

commit v6 on v5

--- a/solution.py
+++ b/solution.py
@@ -298,8 +298,8 @@
     for p in range(8):
         t_rows(0, p, ct[0, p + 1])
     start_y(t_y(0))
-    for j in range(2):
-        for d in range(4):
+    for d in range(4):
+        for j in range(2):
             swap_copy(0, j, d).start()
     for a in range(1, 4):
         pass_on(a)
@@ -354,7 +354,7 @@
         t_step(0, s < 0)
         tables(2 * s)
 
-        @pl.when(s == 0)
+        @pl.when((s == 0) & passing)
         def _():
             pass_on(4)
 
@@ -364,6 +364,12 @@
         return carry
 
     lax.fori_loop(0, STEPS // 2, t_two, 0)
+
+    @pl.when(jnp.logical_not(passing))
+    def _():
+        for g in range(2):
+            arrived(landing(4, g), in_r.at[4, g])
+
     passed_on(range(1, 5))
 
     for p in range(8):
@@ -392,8 +398,8 @@
         start_y(sg_y(cc))
         for copy in sg_x(cc):
             copy.start()
-    for j in range(2):
-        for d in range(4):
+    for d in range(4):
+        for j in range(2):
             swap_copy(1, j, d).start()
 
     jj = iota((128, 128), 0)

time: 141 us -> 141 us (level)
  the two profiles are of different devices: /device:TPU:17 before, /device:TPU:9 now
where the time goes in v6:
time: 141 us
  Pallas kernels  138 us (98%)
  local copies, waits for them, and re-layouts  2.14 us (2%)
    pallas_call x1, Pallas kernels, on_device(): pl.pallas_call(kernel, out_shape=(jax.ShapeDtypeStruct((2, 128, 128), F32...  138 us

profile of v6, /device:TPU:9, one launch (start us, length us, event | category | flops | bytes accessed | tf_op | source)
XLA Modules:
  0.0 141.0 jit_solution(135209537191356096)
XLA Ops:
  0.6 138.2 %survey_gradient.1 = (f32[2,128,128]{2,1,0:T(8,128)}, f32[2,64]{1,0:T(2,128)}) custom-call(f32[2,128,128]{2,1,0:T(8,128)} %conc.1, bf16[3,2,128,128]{3,2,1,0:T(8,128)(2,1)} %vel.1, f32[2,128,128]{2,1,0:T(8,128)} %poro.1, s32[4,16]{1,0:T(4,128)} %bitcast.2, s32[2,2]{1,0:T(2,128)} %sources.1, s32[2,2,64]{2,1,0:T(2,128)} %bitcast.3, f32[2,64]{1,0:T(2,128)} %observed.1, ...), custom_call_target="tpu_custom_call" | custom-call | tf_op jit(solution)/shard_map/survey_gradient/pallas_call | solution.py:710
  138.9 0.0 copy-start
  138.9 1.6 %copy.13 = f32[2,128,128]{2,1,0:T(8,128)} copy(f32[2,128,128]{2,1,0:T(8,128)} %get-tuple-element.4) | data formatting | bytes 262144
  140.5 0.0 copy-done
  140.5 0.6 copy.14
Async XLA Ops:
  138.9 1.6 %copy-start = (f32[2,64]{1,0:T(2,128)S(1)}, f32[2,64]{1,0:T(2,128)}, u32[]{:S(2)}) copy-start(f32[2,64]{1,0:T(2,128)} %get-tuple-element.5) | copy-start | bytes 1540
